TPU v7x, 256 devices: a whole 4x4x8 slice. The times are simulated.
256 devices in a mesh: comp: 2 (over core), blk: 128 (over x, y, z).
Axes of the slice: x: 4, y: 4, z: 8, core: 2. Of those that a mesh axis runs over, the one named last changes fastest.
Arguments:
- conserved: float32 [2, 8, 8192, 512], P('comp', None, 'blk'), may hold values from -3 to 10, as said below
- block_rate: float32 [2, 8192], P('comp', 'blk'), may hold values from 0.004 to 0.016
- neighbours: int32 [2, 8192, 6], P('comp', 'blk'), may hold values from -1 to 8191, as said below
- shell_cell: int32 [2, 128, 128, 32], P('comp', 'blk'), may hold values from 0 to 32694, as said below
- shell_frac: float32 [2, 3, 128, 128, 32], P('comp', None, 'blk'), may hold values from 0 to 1
- shell_target: int32 [2, 128, 128, 32], P('comp', 'blk'), may hold values from 0 to 32768, as said below
Outputs:
- new_state: float32 [2, 8, 8192, 512], P('comp', None, 'blk')
Inputs may be any that keep to these rules, and one draw needn't show every extreme that they name: `conserved`: cells of states whose density and pressure lie between 0.5 and 2 and whose speeds and field components are of order one, with total energy = pressure / (5/3 - 1) + kinetic + magnetic energy. Face neighbours are mutual: if block h is the high-side neighbour of g along an axis, g is the low-side neighbour of h. A neighbour lies on the same device or at most 4 devices away along blk. For each component, axis and each k in -4..-1, 1..4, exactly 3 local block positions of every device have their high-side neighbour k devices away (the same positions on every device); the neighbour is -1 where that device does not exist. So a device sends exactly 18 faces to each device k places away when both exist. `shell_cell`: each stencil lies inside one block: the corner cell has coordinates 0 to 6 along every axis. `shell_target`: for each target component, the used slots of one target device name distinct cells of its blocks, and used slots come first in each row. Every source device fills all 32 slots towards a few target devices and at least half of them towards each of the others.
All inputs are finite; a program needn't handle non-finite values.
Results may differ from a plain program's by a relative error of at most 0.0003.
Values sent between devices are 32-bit elements; how exact they have to be, the bound alone decides.
A program may use at most 256 MiB of HBM per device.

v0:
```python
import jax
import jax.numpy as jnp
import numpy as np
from jax import lax
from jax.sharding import PartitionSpec as P

STEPS = 3
REACH = 4
SLOTS = 18
SHELL_SLOTS = 32


GAMMA = 5.0 / 3.0


def shifted(value, axis, steps):
    count = lax.axis_size(axis)
    leading, last = (max(0, -steps), min(count, count - steps))
    return lax.ppermute(value, axis, [(source, source + steps) for source in range(leading, last)])


def from_partner(block, axis, apart):
    count = lax.axis_size(axis)
    route = []
    for low in range(count):
        high = low | 1 << apart
        if high != low and high < count:
            route += [(low, high), (high, low)]
    return lax.ppermute(block, axis, route)


def wave_flux(u, d):
    inverse = 1.0 / u[0]
    velocity = [u[1] * inverse, u[2] * inverse, u[3] * inverse]
    magnetic_field = [u[4], u[5], u[6]]
    kinetic = 0.5 * (u[1] * velocity[0] + u[2] * velocity[1] + u[3] * velocity[2])
    magnetic = 0.5 * (u[4] * u[4] + u[5] * u[5] + u[6] * u[6])
    pressure = (GAMMA - 1.0) * (u[7] - kinetic - magnetic)
    summed = pressure + magnetic
    normal = velocity[d]
    normal_field = magnetic_field[d]
    alignment = velocity[0] * u[4] + velocity[1] * u[5] + velocity[2] * u[6]
    components = [u[1 + d]]
    for j in range(3):
        component = u[1 + j] * normal - magnetic_field[j] * normal_field
        if j == d:
            component = component + summed
        components.append(component)
    for j in range(3):
        components.append(normal * magnetic_field[j] - normal_field * velocity[j])
    components.append((u[7] + summed) * normal - normal_field * alignment)
    sound_sq = GAMMA * pressure * inverse
    alfven = 2.0 * magnetic * inverse
    combined = sound_sq + alfven
    fast_speed = jnp.sqrt(
        0.5
        * (
            combined
            + jnp.sqrt(combined * combined - 4.0 * sound_sq * normal_field * normal_field * inverse)
        )
    )
    return (jnp.stack(components), jnp.abs(normal) + fast_speed)


def collect_faces(current):
    number = current.shape[1]
    cube = current.reshape(8, number, 8, 8, 8)
    pieces = []
    for f in range(6):
        face = lax.index_in_dim(cube, 7 * (f % 2), 2 + f // 2, keepdims=False)
        pieces.append(face.transpose(1, 0, 2, 3).reshape(number, 512))
    return jnp.concatenate(pieces, axis=0)


def advance(current, ghost_rows, block_rate):
    number = current.shape[1]
    cube = current.reshape(8, number, 8, 8, 8)
    ghosts = ghost_rows.reshape(6, number, 8, 8, 8).transpose(0, 2, 1, 3, 4)
    change = jnp.zeros_like(cube)
    for d in range(3):
        place = 2 + d
        flux_here, speed_here = wave_flux(cube, d)
        ghost_low = jnp.expand_dims(ghosts[2 * d], place)
        ghost_high = jnp.expand_dims(ghosts[2 * d + 1], place)
        flux_low, speed_low = wave_flux(ghost_low, d)
        flux_high, speed_high = wave_flux(ghost_high, d)
        right_state = jnp.concatenate(
            [lax.slice_in_dim(cube, 1, 8, axis=place), ghost_high], axis=place
        )
        right_flux = jnp.concatenate(
            [lax.slice_in_dim(flux_here, 1, 8, axis=place), flux_high], axis=place
        )
        right_speed = jnp.concatenate(
            [lax.slice_in_dim(speed_here, 1, 8, axis=place - 1), speed_high], axis=place - 1
        )
        upper_flux = 0.5 * (flux_here + right_flux) - 0.5 * jnp.maximum(speed_here, right_speed) * (
            right_state - cube
        )
        face_state = lax.slice_in_dim(cube, 0, 1, axis=place)
        face_flux = lax.slice_in_dim(flux_here, 0, 1, axis=place)
        face_speed = lax.slice_in_dim(speed_here, 0, 1, axis=place - 1)
        edge_flux = 0.5 * (flux_low + face_flux) - 0.5 * jnp.maximum(speed_low, face_speed) * (
            face_state - ghost_low
        )
        lower_flux = jnp.concatenate(
            [edge_flux, lax.slice_in_dim(upper_flux, 0, 7, axis=place)], axis=place
        )
        change = change + (upper_flux - lower_flux)
    result = cube - block_rate[None, :, None, None, None] * change
    return result.reshape(8, number, 512)


def interpolate(flattened, cell_index, fractions):
    summed = None
    for a in range(2):
        for b in range(2):
            for c in range(2):
                weight = (
                    (fractions[0] if a else 1.0 - fractions[0])
                    * (fractions[1] if b else 1.0 - fractions[1])
                    * (fractions[2] if c else 1.0 - fractions[2])
                )
                corner = weight * jnp.take(flattened, cell_index + (64 * a + 8 * b + c), axis=1)
                summed = corner if summed is None else summed + corner
    return summed


def offset_slot(offset):
    return jnp.where(offset < 0, offset + REACH, offset + REACH - 1)


def ghost_plan(links, device, number):
    partner = links.T
    face_ids = jnp.arange(6, dtype=jnp.int32)[:, None]
    blocks = jnp.arange(number, dtype=jnp.int32)[None, :]
    linked = (partner >= 0).reshape(-1)
    safe_partner = jnp.where(partner >= 0, partner, 0)
    owners = safe_partner // number
    flat_offset = jnp.where(partner >= 0, owners - device, 0).reshape(-1)
    flat_remote = flat_offset != 0
    flat_entry = (face_ids * number + blocks).reshape(-1)
    flat_theirs = (jnp.bitwise_xor(face_ids, 1) * number + safe_partner % number).reshape(-1)
    same = (flat_offset[:, None] == flat_offset[None, :]) & flat_remote[None, :]
    send_rank = jnp.sum(same & (flat_entry[None, :] < flat_entry[:, None]), axis=1)
    receive_rank = jnp.sum(same & (flat_theirs[None, :] < flat_theirs[:, None]), axis=1)
    offsets = np.concatenate([np.arange(-REACH, 0), np.arange(1, REACH + 1)])
    matches = (
        (flat_offset[None, None, :] == jnp.asarray(offsets, dtype=jnp.int32)[:, None, None])
        & flat_remote[None, None, :]
        & (send_rank[None, None, :] == jnp.arange(SLOTS)[None, :, None])
    )
    found = jnp.any(matches, axis=2)
    picked = jnp.sum(jnp.where(matches, flat_entry[None, None, :], 0), axis=2)
    outgoing_index = jnp.where(found, picked, 6 * number)
    remote_index = 6 * number + 1 + offset_slot(-flat_offset) * SLOTS + receive_rank
    sources = jnp.where(linked, jnp.where(flat_remote, remote_index, flat_theirs), flat_entry)
    return (sources, outgoing_index)


def deliver(outgoing):
    offsets = list(range(-REACH, 0)) + list(range(1, REACH + 1))
    arrivals = []
    for o in range(2 * REACH):
        arrivals.append(shifted(outgoing[o], "blk", offsets[o]))
    return jnp.stack(arrivals)


def on_device(conserved, block_rate, neighbours, shell_cell, shell_frac, shell_target):
    current = conserved[0]
    number = current.shape[1]
    peer_count = lax.axis_size("blk")
    device = lax.axis_index("blk")
    flattened = current.reshape(8, number * 512)
    values = interpolate(flattened, shell_cell[0, 0], shell_frac[0, :, 0])
    bucket = values.transpose(1, 0, 2).reshape(peer_count, 8 * SHELL_SLOTS)
    arrived = lax.all_to_all(bucket, "blk", split_axis=0, concat_axis=0, tiled=True)
    arrived = from_partner(arrived, "comp", 0)
    arrived = (
        arrived.reshape(peer_count, 8, SHELL_SLOTS)
        .transpose(1, 0, 2)
        .reshape(8, peer_count * SHELL_SLOTS)
    )
    current = (
        flattened.at[:, shell_target[0, 0].reshape(-1)]
        .set(arrived, mode="drop")
        .reshape(8, number, 512)
    )
    sources, outgoing_index = ghost_plan(neighbours[0], device, number)
    rates_here = block_rate[0]
    for _ in range(STEPS):
        face_table = jnp.concatenate(
            [collect_faces(current), jnp.zeros((1, 512), jnp.float32)], axis=0
        )
        outgoing = jnp.take(face_table, outgoing_index, axis=0)
        received = deliver(outgoing)
        pooled = jnp.concatenate([face_table, received.reshape(-1, 512)], axis=0)
        ghost_rows = jnp.take(pooled, sources, axis=0)
        current = advance(current, ghost_rows, rates_here)
    return current[None]


def solution(mesh):
    return jax.shard_map(
        on_device,
        mesh=mesh,
        in_specs=(
            P("comp", None, "blk", None),
            P("comp", "blk"),
            P("comp", "blk", None),
            P("comp", "blk", None, None),
            P("comp", None, "blk", None, None),
            P("comp", "blk", None, None),
        ),
        out_specs=P("comp", None, "blk", None),
        check_vma=False,
    )
```

profile of v0, /device:TPU:2, one launch (start us, length us, event | category | flops | bytes accessed | tf_op | source)
XLA Modules:
  0.0 1362.3 jit_solution(1657575151447391939)
XLA Ops:
  6.4 8.7 copy.45530
  15.1 19.8 %gather_fusion.7 = f32[4096,8]{1,0:T(8,128)} fusion(f32[8,32768]{0,1:T(8,128)} %bitcast.3155, s32[4096]{0:T(1024)S(1)} %get-tuple-element.477), kind=kCustom, calls=%fused_computation.9.clone | custom fusion | bytes 278528 | tf_op jit(solution)/shard_map/jit(_take)/gather | solution.py:123
  34.9 19.8 %gather_fusion.6 = f32[4096,8]{1,0:T(8,128)} fusion(f32[8,32768]{0,1:T(8,128)} %bitcast.3156, s32[4096]{0:T(1024)S(1)} %get-tuple-element.478), kind=kCustom, calls=%fused_computation.8.clone | custom fusion | bytes 278528 | tf_op jit(solution)/shard_map/jit(_take)/gather | solution.py:123
  54.8 19.8 %gather_fusion.5 = f32[4096,8]{1,0:T(8,128)} fusion(f32[8,32768]{0,1:T(8,128)} %bitcast.3157, s32[4096]{0:T(1024)S(1)} %get-tuple-element.479), kind=kCustom, calls=%fused_computation.7.clone | custom fusion | bytes 278528 | tf_op jit(solution)/shard_map/jit(_take)/gather | solution.py:123
  74.6 19.8 %gather_fusion.4 = f32[4096,8]{1,0:T(8,128)} fusion(f32[8,32768]{0,1:T(8,128)} %bitcast.3158, s32[4096]{0:T(1024)S(1)} %get-tuple-element.480), kind=kCustom, calls=%fused_computation.6.clone | custom fusion | bytes 278528 | tf_op jit(solution)/shard_map/jit(_take)/gather | solution.py:123
  94.4 19.8 %gather_fusion.3 = f32[4096,8]{1,0:T(8,128)} fusion(f32[8,32768]{0,1:T(8,128)} %bitcast.3159, s32[4096]{0:T(1024)S(1)} %get-tuple-element.481), kind=kCustom, calls=%fused_computation.5.clone | custom fusion | bytes 278528 | tf_op jit(solution)/shard_map/jit(_take)/gather | solution.py:123
  114.3 19.9 %gather_fusion.2 = f32[4096,8]{1,0:T(8,128)} fusion(f32[8,32768]{0,1:T(8,128)} %bitcast.3160, s32[4096]{0:T(1024)S(1)} %get-tuple-element.482), kind=kCustom, calls=%fused_computation.4.clone | custom fusion | bytes 278528 | tf_op jit(solution)/shard_map/jit(_take)/gather | solution.py:123
  134.1 19.8 %gather_fusion.1 = f32[4096,8]{1,0:T(8,128)} fusion(f32[8,32768]{0,1:T(8,128)} %bitcast.3161, s32[4096]{0:T(1024)S(1)} %get-tuple-element.483), kind=kCustom, calls=%fused_computation.3.clone | custom fusion | bytes 278528 | tf_op jit(solution)/shard_map/jit(_take)/gather | solution.py:123
  153.9 19.8 %gather_fusion = f32[4096,8]{1,0:T(8,128)} fusion(f32[8,32768]{0,1:T(8,128)} %bitcast.3162, s32[4096]{0:T(1024)S(1)} %get-tuple-element.484), kind=kCustom, calls=%fused_computation.clone | custom fusion | bytes 278528 | tf_op jit(solution)/shard_map/jit(_take)/gather | solution.py:123
  173.8 13.6 fusion.9
  189.5 15.5 %all-to-all-start = ((f32[128,1,256]{2,1,0:T(1,128)}), f32[128,1,256]{2,1,0:T(1,128)S(1)}, u32[]{:S(2)}, u32[]{:S(2)}) async-start(f32[128,1,256]{2,1,0:T(1,128)} %copy.45557), calls=%async_computation | async-start | bytes 262144 | tf_op jit(solution)/shard_map/all_to_all | solution.py:176
  207.2 9.0 all-to-all-done
  218.8 22.3 %scatter_fusion = f32[8,32768]{0,1:T(8,128)} fusion(f32[8,32768]{0,1:T(8,128)} %bitcast.3163, s32[4096]{0:T(1024)S(1)} %bitcast.3637, f32[4096,8]{1,0:T(8,128)S(1)} %copy.45560), kind=kCustom, calls=%fused_computation.14 | custom fusion | bytes 409600 | tf_op jit(solution)/shard_map/scatter | solution.py:185
  241.0 77.8 %slice_reduce_fusion.4 = (f32[32768]{0:T(1024)S(1)}, f32[32768]{0:T(1024)S(1)}, f32[32768]{0:T(1024)S(1)}, f32[32768]{0:T(1024)S(1)}, f32[32768]{0:T(1024)S(1)},...) fusion(f32[8,32768]{0,1:T(8,128)} %scatter_fusion), kind=kLoop, calls=%fused_computation.19 | loop fusion | flops 32768 | bytes 2097152 | tf_op jit(solution)/shard_map/slice | solution.py:38
  328.4 12.3 copy.45593
  390.7 15.8 %fusion.652 = (f32[8,64,8,8,1]{0,4,3,2,1:T(1,128)}, f32[8,64,8,8,1]{0,4,3,2,1:T(1,128)}) fusion(f32[8,64,8,8,8]{0,4,3,2,1:T(8,128)} %bitcast.3167), kind=kLoop, calls=%fused_computation.1636 | loop fusion | bytes 524288 | tf_op jit(solution)/shard_map/slice | solution.py:70
  406.6 10.8 copy.45934
  531.7 7.8 collective-permute-start.1
  560.7 7.7 collective-permute-start.3
  570.1 10.2 collective-permute-start.4
  717.4 8.3 multiply_subtract_fusion.4
  793.7 7.8 collective-permute-start.16
  812.4 9.9 collective-permute-start.10
  824.4 9.0 collective-permute-start.11
  835.2 7.9 collective-permute-start.12
  845.7 6.8 concatenate.327
  926.6 7.6 multiply_subtract_fusion
  1061.1 7.0 collective-permute-start.24
  1078.4 9.9 collective-permute-start.18
  1090.7 8.8 collective-permute-start.19
  1101.2 8.0 collective-permute-start.20
  1347.3 14.5 %multiply_subtract_fusion.8 = f32[1,8,64,512]{3,2,1,0:T(8,128)} fusion(f32[1,8,64,512]{3,2,1,0:T(8,128)} %copy.46376, f32[1,8,64,512]{3,2,1,0:T(8,128)} %copy.46297, f32[1,8,64,512]{3,2,1,0:T(8,128)} %constant_dynamic-update-slice_fusion.298, f32[1,8,64,512]{3,2,1,0:T(8,128)} %copy.46285, f32[1,8,64,512]{3,2,1,0:T(8,128)} %copy.46229, ...), kind=kLoop, calls=%fused_computation.109 | loop fusion | flops 17301504 | bytes 41025792 | tf_op jit(solution)/shard_map/sub | solution.py:109
  (1223 shorter events, 882.6 us)
Async XLA Ops:
  189.5 26.7 %all-to-all-start = ((f32[128,1,256]{2,1,0:T(1,128)}), f32[128,1,256]{2,1,0:T(1,128)S(1)}, u32[]{:S(2)}, u32[]{:S(2)}) async-start(f32[128,1,256]{2,1,0:T(1,128)} %copy.45557), calls=%async_computation | async-start | bytes 262144 | tf_op jit(solution)/shard_map/all_to_all | solution.py:176
  216.3 1.4 collective-permute-start
  217.0 538.4 %copy-start.208 = (pred[8,18]{1,0:T(8,128)(4,1)}, pred[8,18]{1,0:T(8,128)(4,1)S(1)}, u32[]{:S(2)}) copy-start(pred[8,18]{1,0:T(8,128)(4,1)S(1)} %copy.45601) | copy-start | bytes 436
  217.2 537.4 %copy-start.197 = (s32[1024]{0:T(1024)}, s32[1024]{0:T(1024)S(1)}, u32[]{:S(2)}) copy-start(s32[1024]{0:T(1024)S(1)} %get-tuple-element.486) | copy-start | bytes 12292
  217.2 635.3 %copy-start.206 = (s32[1024]{0:T(1024)}, s32[1024]{0:T(1024)S(1)}, u32[]{:S(2)}) copy-start(s32[1024]{0:T(1024)S(1)} %get-tuple-element.485) | copy-start | bytes 12292
  512.2 333.5 %copy-start.195 = (f32[1,512]{1,0:T(1,128)}, f32[1,512]{1,0:T(1,128)S(1)}, u32[]{:S(2)}) copy-start(f32[1,512]{1,0:T(1,128)S(1)} %broadcast.3613) | copy-start | bytes 6148
  516.7 65.4 %collective-permute-start.8 = (f32[18,512]{1,0:T(8,128)S(1)}, f32[18,512]{1,0:T(8,128)S(1)}, u32[]{:S(2)}, u32[]{:S(2)}) collective-permute-start(f32[18,512]{1,0:T(8,128)S(1)} %get-tuple-element.426), channel_id=1, source_target_pairs={{0,4},{1,5},{2,6},{3,7},{4,8},{5,9},{6,10},{7,11},{8,12},{9,13},{1... | collective-permute-start | bytes 110600 | tf_op jit(solution)/shard_map/ppermute | solution.py:19
  519.9 62.2 %collective-permute-start.7 = (f32[18,512]{1,0:T(8,128)S(1)}, f32[18,512]{1,0:T(8,128)S(1)}, u32[]{:S(2)}, u32[]{:S(2)}) collective-permute-start(f32[18,512]{1,0:T(8,128)S(1)} %get-tuple-element.427), channel_id=1, source_target_pairs={{0,3},{1,4},{2,5},{3,6},{4,7},{5,8},{6,9},{7,10},{8,11},{9,12},{10... | collective-permute-start | bytes 110600 | tf_op jit(solution)/shard_map/ppermute | solution.py:19
  524.9 57.3 %collective-permute-start.6 = (f32[18,512]{1,0:T(8,128)S(1)}, f32[18,512]{1,0:T(8,128)S(1)}, u32[]{:S(2)}, u32[]{:S(2)}) collective-permute-start(f32[18,512]{1,0:T(8,128)S(1)} %get-tuple-element.428), channel_id=1, source_target_pairs={{0,2},{1,3},{2,4},{3,5},{4,6},{5,7},{6,8},{7,9},{8,10},{9,11},{10,... | collective-permute-start | bytes 110600 | tf_op jit(solution)/shard_map/ppermute | solution.py:19
  529.1 53.0 %collective-permute-start.5 = (f32[18,512]{1,0:T(8,128)S(1)}, f32[18,512]{1,0:T(8,128)S(1)}, u32[]{:S(2)}, u32[]{:S(2)}) collective-permute-start(f32[18,512]{1,0:T(8,128)S(1)} %get-tuple-element.429), channel_id=1, source_target_pairs={{0,1},{1,2},{2,3},{3,4},{4,5},{5,6},{6,7},{7,8},{8,9},{9,10},{10,1... | collective-permute-start | bytes 110600 | tf_op jit(solution)/shard_map/ppermute | solution.py:19
  531.7 20.7 %collective-permute-start.1 = (f32[18,512]{1,0:T(8,128)S(1)}, f32[18,512]{1,0:T(8,128)S(1)}, u32[]{:S(2)}, u32[]{:S(2)}) collective-permute-start(f32[18,512]{1,0:T(8,128)S(1)} %get-tuple-element.433), channel_id=1, source_target_pairs={{4,0},{5,1},{6,2},{7,3},{8,4},{9,5},{10,6},{11,7},{12,8},{13,9},{1... | collective-permute-start | bytes 110600 | tf_op jit(solution)/shard_map/ppermute | solution.py:19
  552.4 8.3 collective-permute-start.2
  560.7 9.4 collective-permute-start.3
  570.1 12.0 collective-permute-start.4
  725.7 200.1 %copy-start = (f32[8,64,8,8,8]{1,4,3,2,0:T(8,128)}, f32[8,64,8,8,8]{1,4,3,2,0:T(8,128)S(1)}, u32[]{:S(2)}) copy-start(f32[8,64,8,8,8]{1,4,3,2,0:T(8,128)S(1)} %get-tuple-element.175) | copy-start | bytes 3145732
  755.5 56.2 %collective-permute-start.9 = (f32[18,512]{1,0:T(8,128)S(1)}, f32[18,512]{1,0:T(8,128)S(1)}, u32[]{:S(2)}, u32[]{:S(2)}) collective-permute-start(f32[18,512]{1,0:T(8,128)S(1)} %get-tuple-element.425), channel_id=1, source_target_pairs={{4,0},{5,1},{6,2},{7,3},{8,4},{9,5},{10,6},{11,7},{12,8},{13,9},{1... | collective-permute-start | bytes 110600 | tf_op jit(solution)/shard_map/ppermute | solution.py:19
  793.7 51.3 %collective-permute-start.16 = (f32[18,512]{1,0:T(8,128)S(1)}, f32[18,512]{1,0:T(8,128)S(1)}, u32[]{:S(2)}, u32[]{:S(2)}) collective-permute-start(f32[18,512]{1,0:T(8,128)S(1)} %get-tuple-element.418), channel_id=1, source_target_pairs={{0,4},{1,5},{2,6},{3,7},{4,8},{5,9},{6,10},{7,11},{8,12},{9,13},{1... | collective-permute-start | bytes 110600 | tf_op jit(solution)/shard_map/ppermute | solution.py:19
  801.5 43.4 %collective-permute-start.15 = (f32[18,512]{1,0:T(8,128)S(1)}, f32[18,512]{1,0:T(8,128)S(1)}, u32[]{:S(2)}, u32[]{:S(2)}) collective-permute-start(f32[18,512]{1,0:T(8,128)S(1)} %get-tuple-element.419), channel_id=1, source_target_pairs={{0,3},{1,4},{2,5},{3,6},{4,7},{5,8},{6,9},{7,10},{8,11},{9,12},{10... | collective-permute-start | bytes 110600 | tf_op jit(solution)/shard_map/ppermute | solution.py:19
  807.3 37.6 %collective-permute-start.14 = (f32[18,512]{1,0:T(8,128)S(1)}, f32[18,512]{1,0:T(8,128)S(1)}, u32[]{:S(2)}, u32[]{:S(2)}) collective-permute-start(f32[18,512]{1,0:T(8,128)S(1)} %get-tuple-element.420), channel_id=1, source_target_pairs={{0,2},{1,3},{2,4},{3,5},{4,6},{5,7},{6,8},{7,9},{8,10},{9,11},{10,... | collective-permute-start | bytes 110600 | tf_op jit(solution)/shard_map/ppermute | solution.py:19
  809.2 35.6 %collective-permute-start.13 = (f32[18,512]{1,0:T(8,128)S(1)}, f32[18,512]{1,0:T(8,128)S(1)}, u32[]{:S(2)}, u32[]{:S(2)}) collective-permute-start(f32[18,512]{1,0:T(8,128)S(1)} %get-tuple-element.421), channel_id=1, source_target_pairs={{0,1},{1,2},{2,3},{3,4},{4,5},{5,6},{6,7},{7,8},{8,9},{9,10},{10,1... | collective-permute-start | bytes 110600 | tf_op jit(solution)/shard_map/ppermute | solution.py:19
  812.4 12.1 collective-permute-start.10
  824.4 10.7 collective-permute-start.11
  835.2 9.7 collective-permute-start.12
  1006.8 71.5 %collective-permute-start.17 = (f32[18,512]{1,0:T(8,128)}, f32[18,512]{1,0:T(8,128)}, u32[]{:S(2)}, u32[]{:S(2)}) collective-permute-start(f32[18,512]{1,0:T(8,128)} %get-tuple-element.417), channel_id=1, source_target_pairs={{4,0},{5,1},{6,2},{7,3},{8,4},{9,5},{10,6},{11,7},{12,8},{13,9},{1... | collective-permute-start | bytes 110600 | tf_op jit(solution)/shard_map/ppermute | solution.py:19
  1061.1 57.3 %copy-start.207 = (s32[1024]{0:T(1024)S(1)}, s32[1024]{0:T(1024)}, u32[]{:S(2)}) copy-start(s32[1024]{0:T(1024)} %copy-done.206) | copy-start | bytes 12292
  1061.1 49.9 %collective-permute-start.24 = (f32[18,512]{1,0:T(8,128)S(1)}, f32[18,512]{1,0:T(8,128)S(1)}, u32[]{:S(2)}, u32[]{:S(2)}) collective-permute-start(f32[18,512]{1,0:T(8,128)S(1)} %get-tuple-element.410), channel_id=1, source_target_pairs={{0,4},{1,5},{2,6},{3,7},{4,8},{5,9},{6,10},{7,11},{8,12},{9,13},{1... | collective-permute-start | bytes 110600 | tf_op jit(solution)/shard_map/ppermute | solution.py:19
  1068.1 42.9 %collective-permute-start.23 = (f32[18,512]{1,0:T(8,128)S(1)}, f32[18,512]{1,0:T(8,128)S(1)}, u32[]{:S(2)}, u32[]{:S(2)}) collective-permute-start(f32[18,512]{1,0:T(8,128)S(1)} %copy-done.199), channel_id=1, source_target_pairs={{0,3},{1,4},{2,5},{3,6},{4,7},{5,8},{6,9},{7,10},{8,11},{9,12},{10... | collective-permute-start | bytes 110600 | tf_op jit(solution)/shard_map/ppermute | solution.py:19
  1073.9 37.0 %collective-permute-start.22 = (f32[18,512]{1,0:T(8,128)S(1)}, f32[18,512]{1,0:T(8,128)S(1)}, u32[]{:S(2)}, u32[]{:S(2)}) collective-permute-start(f32[18,512]{1,0:T(8,128)S(1)} %copy-done.200), channel_id=1, source_target_pairs={{0,2},{1,3},{2,4},{3,5},{4,6},{5,7},{6,8},{7,9},{8,10},{9,11},{10,... | collective-permute-start | bytes 110600 | tf_op jit(solution)/shard_map/ppermute | solution.py:19
  1075.8 35.1 %collective-permute-start.21 = (f32[18,512]{1,0:T(8,128)S(1)}, f32[18,512]{1,0:T(8,128)S(1)}, u32[]{:S(2)}, u32[]{:S(2)}) collective-permute-start(f32[18,512]{1,0:T(8,128)S(1)} %copy-done.201), channel_id=1, source_target_pairs={{0,1},{1,2},{2,3},{3,4},{4,5},{5,6},{6,7},{7,8},{8,9},{9,10},{10,1... | collective-permute-start | bytes 110600 | tf_op jit(solution)/shard_map/ppermute | solution.py:19
  1078.4 12.3 collective-permute-start.18
  1090.7 10.5 collective-permute-start.19
  1101.2 9.7 collective-permute-start.20
  (217 other events, 1882.7 us)
where the time goes:
time: 1380 us; the launch traced here: 1360 us
  local copies, waits for them, and re-layouts  845 us (61%)
  other arithmetic  332 us (24%)
  starting transfers between devices  155 us (11%)
  waiting for transfers between devices  26.4 us (2%)
    gather x8, local copies, waits for them, and re-layouts, interpolate(): jnp.take(flattened, cell_index + (64 * a + 8 * b + c), axis=1)  159 us
    ppermute x24, starting transfers between devices, shifted(): lax.ppermute(value, axis, [(source, source + steps) for source in range(l...  139 us
    unnamed x538, local copies, waits for them, and re-layouts  103 us
    unnamed x147, other arithmetic  87.1 us
    another operation x57, local copies, waits for them, and re-layouts, wave_flux(): return (jnp.stack(components), jnp.abs(normal) + fast_speed)  81.4 us
    slice x1, other arithmetic, wave_flux(): pressure = (GAMMA - 1.0) * (u[7] - kinetic - magnetic)  77.8 us
    slice x18, local copies, waits for them, and re-layouts, collect_faces(): face = lax.index_in_dim(cube, 7 * (f % 2), 2 + f // 2, keepdims=False)  50.6 us
    div x33, local copies, waits for them, and re-layouts, wave_flux(): inverse = 1.0 / u[0]  36.9 us
  transfers between devices with their start and end apart: 26, of which 11 were waited for; matrix products, arithmetic and copies ran while one was open for 7% of the time, Pallas kernels for 0%

commit v1 on v0

v1 whole, which is shorter than its diff:
```python
import functools

import jax
import jax.numpy as jnp
from jax import lax
from jax.experimental import pallas as pl
from jax.experimental.pallas import tpu as pltpu
from jax.sharding import PartitionSpec as P

MESH = pl.DeviceIdType.MESH
STEPS = 3
REACH = 4
SLOTS = 32
GAMMA = 5.0 / 3.0
OFFSETS = list(range(-REACH, 0)) + list(range(1, REACH + 1))
SEND_ORDER = sorted(range(2 * REACH), key=lambda o: -abs(OFFSETS[o]))
F32, BF16, I32 = jnp.float32, jnp.bfloat16, jnp.int32


def primitives(u):
    inverse = 1.0 / u[0]
    v = [u[1] * inverse, u[2] * inverse, u[3] * inverse]
    kinetic = 0.5 * (u[1] * v[0] + u[2] * v[1] + u[3] * v[2])
    magnetic = 0.5 * (u[4] * u[4] + u[5] * u[5] + u[6] * u[6])
    pressure = (GAMMA - 1.0) * (u[7] - kinetic - magnetic)
    summed = pressure + magnetic
    align = v[0] * u[4] + v[1] * u[5] + v[2] * u[6]
    sound = GAMMA * pressure * inverse
    combined = sound + 2.0 * magnetic * inverse
    four = 4.0 * sound * inverse
    return v, summed, align, combined, four


def half_flux(u, prim, d):
    v, summed, align, combined, four = prim
    b = u[4:7]
    hn, hb = 0.5 * v[d], 0.5 * b[d]
    flux = [0.5 * u[1 + d]]
    for j in range(3):
        part = u[1 + j] * hn - b[j] * hb
        flux.append(part + 0.5 * summed if j == d else part)
    for j in range(3):
        flux.append(jnp.zeros_like(hn) if j == d else hn * b[j] - hb * v[j])
    flux.append((u[7] + summed) * hn - hb * align)
    inner = jnp.maximum(combined * combined - four * b[d] * b[d], 0.0)
    fast = jnp.sqrt(0.5 * (combined + jnp.sqrt(inner)))
    return flux, jnp.abs(hn) + 0.5 * fast


def take_lanes(table, index):
    rows = table.shape[0]
    return jnp.take_along_axis(
        table, jnp.broadcast_to(index, (rows, 128)), axis=1, mode="promise_in_bounds"
    )


def lane_iota(rows=1):
    return lax.broadcasted_iota(I32, (rows, 128), 1)


def kernel(
    nb, cons, rate, nbr, cell, frac, tgt, out,
    u, uhi, ulo, whi, wlo, tbuf, vbuf, msg, recv, oa, pbuf, acc,
    fs, hy, ft, gb, sb, hrecv, rt, idx,
    a_send, a_recv, h_send, h_recv,
):
    comp = lax.axis_index("comp")
    me = lax.axis_index("blk")
    lane = lane_iota()

    def exists(offset):
        return jnp.logical_and(me + offset >= 0, me + offset < nb)

    recv[...] = jnp.zeros_like(recv)
    rt[...] = jnp.zeros_like(rt)

    @pl.loop(0, STEPS)
    def _(s):
        hrecv[s] = jnp.zeros(hrecv.shape[1:], F32)

    barrier = pltpu.get_barrier_semaphore()

    @pl.loop(0, nb)
    def _(q):
        pl.semaphore_signal(barrier, inc=1, device_id=(1 - comp, q), device_id_type=MESH)

    for offset in OFFSETS:
        @pl.when(exists(offset))
        def _():
            pl.semaphore_signal(barrier, inc=1, device_id=(comp, me + offset), device_id_type=MESH)

    for var in range(8):
        for j in range(2):
            low = cons[var, :, 128 * j : 128 * j + 128]
            high = cons[var, :, 128 * j + 256 : 128 * j + 384]
            turned = jnp.concatenate([low, high], axis=0).T
            for k in range(2):
                part = turned[64 * k : 64 * k + 64]
                u[2 * j + k, var] = part
                upper = part.astype(BF16)
                at = (2 * j + k) * 128
                uhi[64 * var : 64 * var + 64, at : at + 128] = upper
                ulo[64 * var : 64 * var + 64, at : at + 128] = (part - upper.astype(F32)).astype(BF16)

    rows512 = lax.broadcasted_iota(I32, (512, 128), 0)
    sub8 = lax.broadcasted_iota(I32, (8, 128), 0)

    def interpolate(g):
        at = pl.multiple_of(g * 8, 8)
        cells = cell[pl.ds(at, 8), :]
        fxs, fys, fzs = (frac[k, pl.ds(at, 8), :] for k in range(3))
        x = (cells >> 6) & 7
        block = cells >> 9
        a0s = (x & 3) * 128 + (x >> 2) * 64 + block
        x1 = x + 1
        a1s = (x1 & 3) * 128 + (x1 >> 2) * 64 + block
        w0 = 1.0 - fxs
        w0h = w0.astype(BF16).astype(F32)
        w0l = w0 - w0h
        w1h = fxs.astype(BF16).astype(F32)
        w1l = fxs - w1h
        ys, zs = (cells >> 3) & 7, cells & 7
        for t in range(8):
            row = slice(t, t + 1)
            first = rows512 == a0s[row]
            second = rows512 == a1s[row]
            whi[:, 128 * t : 128 * t + 128] = jnp.where(
                first, w0h[row], jnp.where(second, w1h[row], 0.0)
            ).astype(BF16)
            wlo[:, 128 * t : 128 * t + 128] = jnp.where(
                first, w0l[row], jnp.where(second, w1l[row], 0.0)
            ).astype(BF16)
        tbuf[...] = (
            jnp.dot(uhi[...], whi[...], preferred_element_type=F32)
            + jnp.dot(ulo[...], whi[...], preferred_element_type=F32)
            + jnp.dot(uhi[...], wlo[...], preferred_element_type=F32)
        )
        for t in range(8):
            row = slice(t, t + 1)
            wz = jnp.where(sub8 == zs[row], 1.0 - fzs[row], jnp.where(sub8 == zs[row] + 1, fzs[row], 0.0))
            wys = []
            for y in range(8):
                wy = jnp.where(ys[row] == y, 1.0 - fys[row], jnp.where(ys[row] + 1 == y, fys[row], 0.0))
                wys.append(wy * wz)
            values = []
            for var in range(8):
                total = None
                for y in range(8):
                    term = wys[y] * tbuf[64 * var + 8 * y : 64 * var + 8 * y + 8, 128 * t : 128 * t + 128]
                    total = term if total is None else total + term
                values.append(jnp.sum(total, axis=0, keepdims=True))
            vbuf[pl.ds(pl.multiple_of(g * 64 + t * 8, 8), 8), :] = jnp.concatenate(values, axis=0)

    for half in range(2):
        @pl.loop(2 * half, 2 * half + 2)
        def _(g):
            interpolate(g)

        msg[half] = vbuf[128 * half : 128 * half + 128, :].T.reshape(128, 1, 128)
        if half == 0:
            near_by = jnp.minimum(me, REACH) + jnp.minimum(nb - 1 - me, REACH)
            pl.semaphore_wait(barrier, nb + near_by)

        @pl.loop(1, nb + 1)
        def _(i):
            q = lax.rem(me + i, nb)
            pltpu.make_async_remote_copy(
                src_ref=msg.at[half, q],
                dst_ref=recv.at[half, me],
                send_sem=a_send.at[half],
                recv_sem=a_recv.at[half],
                device_id=(1 - comp, q),
                device_id_type=MESH,
            ).start()

    targets = tgt[...]
    tx = (targets >> 6) & 7
    ta = jnp.where(
        targets < 64 * 512, (tx & 3) * 128 + (tx >> 2) * 64 + (targets >> 9), -1
    ).astype(F32)
    columns = jnp.concatenate([ta, jnp.zeros((96, 128), F32)], axis=0).T
    lanes512 = lax.broadcasted_iota(I32, (128, 512), 1).astype(F32)
    for s in range(SLOTS):
        oa[128 * s : 128 * s + 128, :] = jnp.where(
            lanes512 == columns[:, s : s + 1], 1.0, 0.0
        ).astype(BF16)

    links = nbr[...]
    links_c = jnp.concatenate([links.astype(F32), jnp.zeros((120, 128), F32)], axis=0).T.astype(I32)
    upper_lanes = lane >> 6
    half_lane = lane & 63
    group = (half_lane * 43) >> 8
    place = half_lane - 6 * group
    block_c = lax.broadcasted_iota(I32, (64, 1), 0)
    origin = {}
    for f in range(6):
        near = links[f : f + 1, :]
        far = links_c[0:64, f : f + 1]
        off_r = jnp.where(near >= 0, (near >> 6) - me, 0)
        off_c = jnp.where(far >= 0, (far >> 6) - me, 0)
        before = jnp.where((off_c == off_r) & ((far & 63) < (near & 63)), 1.0, 0.0)
        rank_r = jnp.sum(before, axis=0, keepdims=True).astype(I32)
        earlier = jnp.where((off_c == off_r) & (lane < block_c), 1.0, 0.0)
        rank_c = jnp.sum(earlier, axis=1, keepdims=True).astype(I32)
        slot_c = jnp.where(off_c < 0, off_c + REACH, off_c + REACH - 1)
        slot_c = jnp.where(off_c == 0, -1, slot_c)
        slot_r = jnp.where(off_r < 0, off_r + REACH, off_r + REACH - 1)
        if f < 2:
            wanted = jnp.where(place >= 3, place - 3, place)
            mine = (place >= 3) if f == 1 else (place < 3)
        else:
            wanted = place >> 1
            mine = place >= 0
        hit = (slot_c == group) & (rank_c == wanted) & mine
        which = jnp.sum(jnp.where(hit, block_c.astype(F32), 0.0), axis=0, keepdims=True).astype(I32)
        origin[f] = (off_r, near, rank_r, slot_r, which)
    side = upper_lanes

    def pick(a, b):
        return jnp.where(side == 0, a, b)

    idx[0:1, :] = jnp.where(place >= 3, 64 + origin[1][4], origin[0][4])
    off_x = pick(origin[0][0], origin[1][0])
    near_x = pick(origin[0][1], origin[1][1])
    rank_x = pick(origin[0][2], origin[1][2])
    slot_x = pick(origin[0][3], origin[1][3])
    idx[3:4, :] = jnp.where(near_x >= 0, (1 - side) * 64 + (near_x & 63), lane)
    idx[4:5, :] = jnp.where(off_x != 0, slot_x * 6 + (1 - side) * 3 + rank_x, -1)
    for d in (1, 2):
        idx[d : d + 1, :] = 64 * (place & 1) + pick(origin[2 * d][4], origin[2 * d + 1][4])
        for high in range(2):
            off, near, rank, slot, _ = origin[2 * d + high]
            at = 5 + 6 * (d - 1) + 3 * high
            idx[at : at + 1, :] = jnp.where(near >= 0, 64 * side + (near & 63), -1)
            idx[at + 1 : at + 2, :] = jnp.where(
                off != 0, slot * 6 + rank * 2 + side + (0 if high else 64), -1
            )

    rows64 = lax.broadcasted_iota(I32, (64, 128), 0)
    for half in range(2):
        whole = recv.at[half, pl.ds(0, nb)]
        pltpu.make_async_copy(whole, whole, a_recv.at[half]).wait()
        vbuf[128 * half : 128 * half + 128, :] = recv[half].reshape(128, 128).T
    acc[...] = jnp.zeros_like(acc)

    @pl.loop(0, 4)
    def _(g):
        places = tgt[pl.ds(pl.multiple_of(g * 8, 8), 8), :] & 63
        for t in range(8):
            value = vbuf[pl.ds(pl.multiple_of(g * 64 + t * 8, 8), 8), :]
            upper = value.astype(BF16).astype(F32)
            lower = value - upper
            here = rows64 == places[t : t + 1]
            cols = slice(128 * t, 128 * t + 128)
            for var in range(8):
                pbuf[64 * var : 64 * var + 64, cols] = jnp.where(here, upper[var : var + 1], 0.0).astype(BF16)
                pbuf[512 + 64 * var : 576 + 64 * var, cols] = jnp.where(here, lower[var : var + 1], 0.0).astype(BF16)
            pbuf[1024:1088, cols] = jnp.where(here, 1.0, 0.0).astype(BF16)
        acc[...] += jnp.dot(
            pbuf[...], oa[pl.ds(pl.multiple_of(g * 1024, 1024), 1024), :], preferred_element_type=F32
        )

    for xl in range(4):
        cols = slice(128 * xl, 128 * xl + 128)
        changed = acc[1024:1088, cols] > 0.5
        for var in range(8):
            rows = slice(64 * var, 64 * var + 64)
            lower = slice(512 + 64 * var, 576 + 64 * var)
            u[xl, var] = jnp.where(changed, acc[rows, cols] + acc[lower, cols], u[xl, var])
    for half in range(2):
        whole = msg.at[half, pl.ds(0, nb)]
        pltpu.make_async_copy(whole, whole, a_send.at[half]).wait()

    rates = rate[...]
    low_lanes = lane_iota(8) < 64
    swap = functools.partial(pltpu.roll, shift=64, axis=1)

    def copy_of(step, pair, o):
        offset = OFFSETS[o]
        return pltpu.make_async_remote_copy(
            src_ref=sb.at[pair, o],
            dst_ref=hrecv.at[step, pair, OFFSETS.index(-offset)],
            send_sem=h_send.at[step, pair, o],
            recv_sem=h_recv.at[step, pair, OFFSETS.index(-offset)],
            device_id=(comp, me + offset),
            device_id_type=MESH,
        )

    def tile(y):
        return pl.ds(pl.multiple_of(y * 8, 8), 8)

    @pl.loop(0, STEPS)
    def _(step):
        for pair in range(3):
            for xl in range(4):
                for var in range(8):
                    at = slice(64 * xl + 8 * var, 64 * xl + 8 * var + 8)
                    if pair == 1:
                        ft[2, at, :] = u[xl, var, 0:8, :]
                        ft[3, at, :] = u[xl, var, 56:64, :]
                    elif pair == 2:
                        ft[4, at, :] = u[xl, var, pl.ds(0, 8, stride=8), :]
                        ft[5, at, :] = u[xl, var, pl.ds(7, 8, stride=8), :]
            if pair == 0:
                for var in range(8):
                    ft[var // 4, 64 * (var % 4) : 64 * (var % 4) + 64, :] = jnp.where(
                        lane < 64, u[0, var], u[3, var]
                    )
            take = idx[pair : pair + 1, :]
            packed = jnp.where(lane < 64, take_lanes(ft[2 * pair], take), take_lanes(ft[2 * pair + 1], take))
            for r in range(2):
                turned = packed[128 * r : 128 * r + 128].T
                for o in range(8):
                    for s in range(2):
                        sb[pair, o, 12 * s + 6 * r : 12 * s + 6 * r + 6, :] = turned[
                            64 * s + 6 * o : 64 * s + 6 * o + 6
                        ]
            for o in SEND_ORDER:
                @pl.when(exists(OFFSETS[o]))
                def _():
                    copy_of(step, pair, o).start()

        @pl.loop(0, 8)
        def _(y):
            for xl in range(4):
                cells = [u[xl, var, tile(y), :] for var in range(8)]
                prim = primitives(cells)
                for d in range(3):
                    flux, speed = half_flux(cells, prim, d)
                    for c in range(8):
                        fs[d, xl, c, tile(y), :] = flux[c]
                    fs[d, xl, 8, tile(y), :] = speed

        hy[...] = jnp.zeros_like(hy)

        @pl.loop(0, 8)
        def _(y):
            here, above = tile(y), tile(jnp.minimum(y + 1, 7))
            keep_y = jnp.where(y < 7, 1.0, 0.0)
            keep_z = sub8 < 7
            sx = [fs[0, xl, 8, here, :] for xl in range(4)]
            mx = [jnp.maximum(sx[xl], sx[xl + 1]) for xl in range(3)]
            mx.append(jnp.maximum(sx[3], swap(sx[0])))
            my, mz = [], []
            for xl in range(4):
                my.append(jnp.maximum(fs[1, xl, 8, here, :], fs[1, xl, 8, above, :]))
                sz = fs[2, xl, 8, here, :]
                mz.append(jnp.maximum(sz, pltpu.roll(sz, 7, 0)))
            for c in range(8):
                state = [u[xl, c, here, :] for xl in range(4)]
                fx = [fs[0, xl, c, here, :] for xl in range(4)]
                hx = []
                for xl in range(3):
                    hx.append(fx[xl] + fx[xl + 1] - mx[xl] * (state[xl + 1] - state[xl]))
                last = fx[3] + swap(fx[0]) - mx[3] * (swap(state[0]) - state[3])
                hx.append(jnp.where(low_lanes, last, 0.0))
                for xl in range(4):
                    change = hx[xl] - (hx[xl - 1] if xl else swap(hx[3]))
                    up = (
                        fs[1, xl, c, here, :] + fs[1, xl, c, above, :]
                        - my[xl] * (u[xl, c, above, :] - state[xl])
                    ) * keep_y
                    change = change + (up - hy[xl, c])
                    hy[xl, c] = up
                    fz = fs[2, xl, c, here, :]
                    right = fz + pltpu.roll(fz, 7, 0) - mz[xl] * (pltpu.roll(state[xl], 7, 0) - state[xl])
                    right = jnp.where(keep_z, right, 0.0)
                    change = change + (right - pltpu.roll(right, 1, 0))
                    u[xl, c, here, :] = state[xl] - rates * change

        def edge(own, ghost, d, sign):
            own_flux, own_speed = half_flux(own, primitives(own), d)
            far_flux, far_speed = half_flux(ghost, primitives(ghost), d)
            most = jnp.maximum(own_speed, far_speed)
            return [
                rates * (sign * (own_flux[c] + far_flux[c]) - most * (own[c] - ghost[c]))
                for c in range(8)
            ]

        for pair in range(3):
            for o in range(8):
                @pl.when(exists(-OFFSETS[o]))
                def _():
                    copy_of(step, pair, o).wait_recv()
            for o in range(8):
                for r in range(2):
                    for s in range(2):
                        rt[r, 64 * s + 6 * o : 64 * s + 6 * o + 6, :] = hrecv[
                            step, pair, o, 12 * s + 6 * r : 12 * s + 6 * r + 6, :
                        ]
            arrived = jnp.concatenate([rt[0].T, rt[1].T], axis=0)
            if pair == 0:
                near = idx[3:4, :]
                far = idx[4:5, :]
                for s in range(2):
                    gb[s] = jnp.where(
                        far >= 0,
                        take_lanes(arrived, jnp.maximum(far, 0) + 64 * s),
                        take_lanes(ft[s], near),
                    )

                @pl.loop(0, 8)
                def _(y):
                    own = [ft[c // 4, pl.ds(pl.multiple_of(64 * (c % 4) + y * 8, 8), 8), :] for c in range(8)]
                    ghost = [gb[c // 4, pl.ds(pl.multiple_of(64 * (c % 4) + y * 8, 8), 8), :] for c in range(8)]
                    delta = edge(own, ghost, 0, jnp.where(low_lanes, 1.0, -1.0))
                    for c in range(8):
                        u[0, c, tile(y), :] = u[0, c, tile(y), :] + jnp.where(low_lanes, delta[c], 0.0)
                        u[3, c, tile(y), :] = u[3, c, tile(y), :] + jnp.where(low_lanes, 0.0, delta[c])
            else:
                for high in range(2):
                    at = 5 + 6 * (pair - 1) + 3 * high
                    near = idx[at : at + 1, :]
                    far = idx[at + 1 : at + 2, :]
                    local = jnp.where(
                        near >= 0,
                        take_lanes(ft[2 * pair + 1 - high], jnp.maximum(near, 0)),
                        ft[2 * pair + high],
                    )
                    gb[high] = jnp.where(far >= 0, take_lanes(arrived, jnp.maximum(far, 0)), local)
                    for xl in range(4):
                        rows = [slice(64 * xl + 8 * c, 64 * xl + 8 * c + 8) for c in range(8)]
                        own = [ft[2 * pair + high, rows[c], :] for c in range(8)]
                        ghost = [gb[high, rows[c], :] for c in range(8)]
                        delta = edge(own, ghost, pair, -1.0 if high else 1.0)
                        for c in range(8):
                            if pair == 1:
                                part = slice(56, 64) if high else slice(0, 8)
                            else:
                                part = pl.ds(7 if high else 0, 8, stride=8)
                            u[xl, c, part, :] = u[xl, c, part, :] + delta[c]

        for pair in range(3):
            for o in range(8):
                @pl.when(exists(OFFSETS[o]))
                def _():
                    copy_of(step, pair, o).wait_send()

    for var in range(8):
        for j in range(2):
            turned = jnp.concatenate([u[2 * j, var], u[2 * j + 1, var]], axis=0).T
            out[var, :, 128 * j : 128 * j + 128] = turned[0:64]
            out[var, :, 128 * j + 256 : 128 * j + 384] = turned[64:128]


def on_device(nb, conserved, block_rate, neighbours, shell_cell, shell_frac, shell_target):
    extra = 128 - nb
    cell = jnp.pad(shell_cell[0, 0].T, ((0, 0), (0, extra)))
    frac = jnp.pad(shell_frac[0, :, 0].transpose(0, 2, 1), ((0, 0), (0, 0), (0, extra)))
    target = jnp.pad(shell_target[0, 0].T, ((0, 0), (0, extra)), constant_values=64 * 512)
    links = neighbours[0].T
    links = jnp.pad(jnp.concatenate([links, links], axis=1), ((0, 2), (0, 0)), constant_values=-1)
    rates = jnp.concatenate([block_rate, block_rate], axis=1)
    vmem = pl.BlockSpec(memory_space=pltpu.VMEM)
    result = pl.pallas_call(
        functools.partial(kernel, nb),
        out_shape=jax.ShapeDtypeStruct((8, 64, 512), F32),
        in_specs=[vmem] * 6,
        out_specs=vmem,
        scratch_shapes=[
            pltpu.VMEM((4, 8, 64, 128), F32),
            pltpu.VMEM((512, 512), BF16),
            pltpu.VMEM((512, 512), BF16),
            pltpu.VMEM((512, 1024), BF16),
            pltpu.VMEM((512, 1024), BF16),
            pltpu.VMEM((512, 1024), F32),
            pltpu.VMEM((256, 128), F32),
            pltpu.VMEM((2, 128, 1, 128), F32),
            pltpu.VMEM((2, 128, 1, 128), F32),
            pltpu.VMEM((4096, 512), BF16),
            pltpu.VMEM((1088, 1024), BF16),
            pltpu.VMEM((1088, 512), F32),
            pltpu.VMEM((3, 4, 9, 64, 128), F32),
            pltpu.VMEM((4, 8, 8, 128), F32),
            pltpu.VMEM((6, 256, 128), F32),
            pltpu.VMEM((2, 256, 128), F32),
            pltpu.VMEM((3, 8, 24, 128), F32),
            pltpu.VMEM((STEPS, 3, 8, 24, 128), F32),
            pltpu.VMEM((2, 128, 128), F32),
            pltpu.VMEM((24, 128), I32),
            pltpu.SemaphoreType.DMA((2,)),
            pltpu.SemaphoreType.DMA((2,)),
            pltpu.SemaphoreType.DMA((STEPS, 3, 8)),
            pltpu.SemaphoreType.DMA((STEPS, 3, 8)),
        ],
        compiler_params=pltpu.CompilerParams(
            collective_id=0, has_side_effects=True, vmem_limit_bytes=48 << 20
        ),
    )(conserved[0], rates, links, cell, frac, target)
    return result[None]


def solution(mesh):
    return jax.shard_map(
        functools.partial(on_device, mesh.shape["blk"]),
        mesh=mesh,
        in_specs=(
            P("comp", None, "blk", None),
            P("comp", "blk"),
            P("comp", "blk", None),
            P("comp", "blk", None, None),
            P("comp", None, "blk", None, None),
            P("comp", "blk", None, None),
        ),
        out_specs=P("comp", None, "blk", None),
        check_vma=False,
    )
```

time: 1380 us -> 76 us (0.06); the launches traced: 1360 us -> 75.7 us
  local copies, waits for them, and re-layouts: 845 us -> 4.34 us
  other arithmetic: 332 us -> 0.15 us
  starting transfers between devices: 155 us -> 0 us
  Pallas kernels: 0 us -> 71.2 us
  waiting for transfers between devices: 26.4 us -> 0 us
    gather x17 -> x0, local copies, waits for them, and re-layouts: 172 us -> none  [the longest x8 159 us: interpolate(): jnp.take(flattened, cell_index + (64 * a + 8 * b + c), axis=1)]
    ppermute x25 -> x0, starting transfers between devices: 139 us -> none  [the longest x24 139 us: shifted(): lax.ppermute(value, axis, [(source, source + steps) for source in range(l...]
    squeeze x75 -> x0, local copies, waits for them, and re-layouts: 122 us -> none  [the longest x22 30.1 us: wave_flux(): component = u[1 + j] * normal - magnetic_field[j] * normal_field]
    concatenate x45 -> x0, local copies, waits for them, and re-layouts: 112 us -> none  [the longest x9 28.5 us: advance(): jnp.concatenate([lax.slice_in_dim(cube, 1, 8, axis=place), ghost_high], a...]
    another operation x67 -> x0, local copies, waits for them, and re-layouts: 108 us -> none  [the longest x57 81.4 us: wave_flux(): return (jnp.stack(components), jnp.abs(normal) + fast_speed)]
    slice x72 -> x0, local copies, waits for them, and re-layouts: 108 us -> none  [the longest x18 50.6 us: collect_faces(): face = lax.index_in_dim(cube, 7 * (f % 2), 2 + f // 2, keepdims=False)]
    unnamed x538 -> x12, local copies, waits for them, and re-layouts: 103 us -> 4.33 us
    unnamed x147 -> x0, other arithmetic: 87.1 us -> none
  transfers between devices with their start and end apart: 26 -> 0, of which waited for: 11 -> 0; matrix products, arithmetic and copies ran while one was open for 7% -> 0% of each run, Pallas kernels for 0% -> 0%
where the time goes in v1:
time: 76 us; the launch traced here: 75.7 us
  Pallas kernels  71.2 us (94%)
  local copies, waits for them, and re-layouts  4.34 us (6%)
    pallas_call x1, Pallas kernels, on_device(): pl.pallas_call(functools.partial(kernel, nb), out_shape=jax.ShapeDtypeStr...  71.2 us
    unnamed x12, local copies, waits for them, and re-layouts  4.33 us

profile of v1, /device:TPU:2, one launch (start us, length us, event | category | flops | bytes accessed | tf_op | source)
XLA Modules:
  0.0 75.7 jit_solution(8306283951266142179)
XLA Ops:
  0.0 0.0 copy-start.4
  0.0 0.0 copy-start.3
  0.0 0.0 copy-start.2
  0.0 0.6 copy-done.4
  0.7 0.1 pad_maximum_fusion.rate
  0.7 0.7 copy.9
  1.4 0.1 pad_add_fusion
  1.5 0.0 copy-done.3
  1.5 0.0 copy-done.2
  1.5 0.0 copy-start
  1.5 1.2 %copy-done = f32[1,8,64,512]{3,2,1,0:T(8,128)S(1)} copy-done((f32[1,8,64,512]{3,2,1,0:T(8,128)S(1)}, f32[1,8,64,512]{3,2,1,0:T(8,128)}, u32[]{:S(2)}) %copy-start) | copy-done | bytes 1048600
  2.7 0.0 copy-start.1
  2.7 0.8 %copy-done.1 = f32[1,3,1,128,32]{3,4,2,1,0:T(8,128)S(1)} copy-done((f32[1,3,1,128,32]{3,4,2,1,0:T(8,128)S(1)}, f32[1,3,1,128,32]{3,4,2,1,0:T(8,128)}, u32[]{:S(2)}) %copy-start.1) | copy-done | bytes 49176
  3.5 71.2 %shard_map.64 = f32[8,64,512]{2,1,0:T(8,128)S(1)} custom-call(f32[8,64,512]{2,1,0:T(8,128)S(1)} %bitcast.17, f32[1,128]{1,0:T(1,128)S(1)} %pad_maximum_fusion.rate, s32[8,128]{1,0:T(8,128)S(1)} %pad.4.nbr, s32[32,128]{1,0:T(8,128)S(1)} %bitcast.19, f32[3,32,128]{2,1,0:T(8,128)S(1)} %bitcast.18, s32[32,128]{1,0:T(8,128)S(1)} %bitcast.20), custom_call_target="tpu_custom_call" | custom-call | tf_op jit(solution)/shard_map/pallas_call | solution.py:455
  74.8 1.0 %copy.11 = f32[1,8,64,512]{3,2,1,0:T(8,128)} copy(f32[1,8,64,512]{3,2,1,0:T(8,128)S(1)} %bitcast.16) | data formatting | bytes 2097152
  (1 shorter events, 0.0 us)
Async XLA Ops:
  0.0 0.7 copy-start.4
  0.0 1.5 %copy-start.3 = (s32[1,1,128,32]{2,3,1,0:T(8,128)S(1)}, s32[1,1,128,32]{2,3,1,0:T(8,128)}, u32[]{:S(2)}) copy-start(s32[1,1,128,32]{2,3,1,0:T(8,128)} %param.11) | copy-start | bytes 49156
  0.0 1.5 %copy-start.2 = (s32[1,1,128,32]{2,3,1,0:T(8,128)S(1)}, s32[1,1,128,32]{2,3,1,0:T(8,128)}, u32[]{:S(2)}) copy-start(s32[1,1,128,32]{2,3,1,0:T(8,128)} %param.9) | copy-start | bytes 49156
  1.5 1.2 %copy-start = (f32[1,8,64,512]{3,2,1,0:T(8,128)S(1)}, f32[1,8,64,512]{3,2,1,0:T(8,128)}, u32[]{:S(2)}) copy-start(f32[1,8,64,512]{3,2,1,0:T(8,128)} %param.6) | copy-start | bytes 3145732
  2.7 0.8 %copy-start.1 = (f32[1,3,1,128,32]{3,4,2,1,0:T(8,128)S(1)}, f32[1,3,1,128,32]{3,4,2,1,0:T(8,128)}, u32[]{:S(2)}) copy-start(f32[1,3,1,128,32]{3,4,2,1,0:T(8,128)} %param.10) | copy-start | bytes 147460

commit v2 on v1

--- a/solution.py
+++ b/solution.py
@@ -59,9 +59,10 @@
 
 
 def kernel(
-    nb, cons, rate, nbr, cell, frac, tgt, out,
-    u, uhi, ulo, whi, wlo, tbuf, vbuf, msg, recv, oa, pbuf, acc,
-    fs, hy, ft, gb, sb, hrecv, rt, idx,
+    nb, cons_hbm, rate_hbm, nbr_hbm, cell_hbm, frac_hbm, tgt_hbm, out,
+    cons, rate, nbr, cell, frac, tgt, links, in_sem,
+    cur, ub, wb, tbuf, vbuf, msg, recv, oa, pbuf, acc,
+    fs, hy, old, ft, gb, sb, hrecv, rt, idx,
     a_send, a_recv, h_send, h_recv,
 ):
     comp = lax.axis_index("comp")
@@ -71,7 +72,17 @@
     def exists(offset):
         return jnp.logical_and(me + offset >= 0, me + offset < nb)
 
-    recv[...] = jnp.zeros_like(recv)
+    loads = [
+        pltpu.make_async_copy(source, held, in_sem.at[k])
+        for k, (source, held) in enumerate(
+            ((cell_hbm, cell), (frac_hbm, frac), (cons_hbm, cons), (tgt_hbm, tgt), (nbr_hbm, nbr), (rate_hbm, rate))
+        )
+    ]
+    for load in loads:
+        load.start()
+
+    if nb < 128:
+        recv[...] = jnp.zeros_like(recv)
     rt[...] = jnp.zeros_like(rt)
 
     @pl.loop(0, STEPS)
@@ -89,6 +100,8 @@
         def _():
             pl.semaphore_signal(barrier, inc=1, device_id=(comp, me + offset), device_id_type=MESH)
 
+    for load in loads:
+        load.wait()
     for var in range(8):
         for j in range(2):
             low = cons[var, :, 128 * j : 128 * j + 128]
@@ -96,52 +109,78 @@
             turned = jnp.concatenate([low, high], axis=0).T
             for k in range(2):
                 part = turned[64 * k : 64 * k + 64]
-                u[2 * j + k, var] = part
+                cur[2 * j + k, var] = part
                 upper = part.astype(BF16)
                 at = (2 * j + k) * 128
-                uhi[64 * var : 64 * var + 64, at : at + 128] = upper
-                ulo[64 * var : 64 * var + 64, at : at + 128] = (part - upper.astype(F32)).astype(BF16)
-
-    rows512 = lax.broadcasted_iota(I32, (512, 128), 0)
+                rows = slice(64 * var, 64 * var + 64)
+                ub[rows, at : at + 128] = upper
+                ub[rows, at + 512 : at + 640] = (part - upper.astype(F32)).astype(BF16)
+                ub[rows, at + 1024 : at + 1152] = upper
+
+    def send_values(half):
+        def send(q):
+            pltpu.make_async_remote_copy(
+                src_ref=msg.at[half, q],
+                dst_ref=recv.at[half, me],
+                send_sem=a_send.at[half],
+                recv_sem=a_recv.at[half],
+                device_id=(1 - comp, q),
+                device_id_type=MESH,
+            ).start()
+
+        if nb == 128:
+            planes = [
+                lax.rem(me // 32 + dx, 4) * 32 + lax.rem(me // 8 + dy, 4) * 8
+                for dx, dy in ((2, 2), (2, 1), (2, 3), (1, 2), (3, 2), (1, 1), (1, 3), (3, 1), (3, 3),
+                               (2, 0), (0, 2), (1, 0), (3, 0), (0, 1), (0, 3), (0, 0))
+            ]
+            height = lax.rem(me, 8)
+
+            @pl.loop(0, 8)
+            def _(j):
+                step = (j + 1) // 2
+                z = lax.rem(height + 4 + step * (1 - 2 * lax.rem(j, 2)), 8)
+                for plane in planes:
+                    send(plane + z)
+        else:
+            @pl.loop(1, nb + 1)
+            def _(i):
+                send(lax.rem(me + i, nb))
+
+    rows64 = lax.broadcasted_iota(I32, (64, 128), 0)
     sub8 = lax.broadcasted_iota(I32, (8, 128), 0)
 
     def interpolate(g):
         at = pl.multiple_of(g * 8, 8)
         cells = cell[pl.ds(at, 8), :]
         fxs, fys, fzs = (frac[k, pl.ds(at, 8), :] for k in range(3))
-        x = (cells >> 6) & 7
-        block = cells >> 9
-        a0s = (x & 3) * 128 + (x >> 2) * 64 + block
-        x1 = x + 1
-        a1s = (x1 & 3) * 128 + (x1 >> 2) * 64 + block
-        w0 = 1.0 - fxs
-        w0h = w0.astype(BF16).astype(F32)
-        w0l = w0 - w0h
-        w1h = fxs.astype(BF16).astype(F32)
-        w1l = fxs - w1h
+        xs = (cells >> 6) & 7
+        blocks = cells >> 9
         ys, zs = (cells >> 3) & 7, cells & 7
+
+        def along(corners, fractions, row):
+            first, part = corners[row], fractions[row]
+            return jnp.where(sub8 == first, 1.0 - part, jnp.where(sub8 == first + 1, part, 0.0))
+
         for t in range(8):
             row = slice(t, t + 1)
-            first = rows512 == a0s[row]
-            second = rows512 == a1s[row]
-            whi[:, 128 * t : 128 * t + 128] = jnp.where(
-                first, w0h[row], jnp.where(second, w1h[row], 0.0)
-            ).astype(BF16)
-            wlo[:, 128 * t : 128 * t + 128] = jnp.where(
-                first, w0l[row], jnp.where(second, w1l[row], 0.0)
-            ).astype(BF16)
-        tbuf[...] = (
-            jnp.dot(uhi[...], whi[...], preferred_element_type=F32)
-            + jnp.dot(ulo[...], whi[...], preferred_element_type=F32)
-            + jnp.dot(uhi[...], wlo[...], preferred_element_type=F32)
-        )
+            cols = slice(128 * t, 128 * t + 128)
+            wx = along(xs, fxs, row)
+            upper = wx.astype(BF16).astype(F32)
+            lower = wx - upper
+            inside = rows64 == blocks[row]
+            for x in range(8):
+                at = (x & 3) * 128 + (x >> 2) * 64
+                part = jnp.where(inside, upper[x : x + 1], 0.0).astype(BF16)
+                wb[at : at + 64, cols] = part
+                wb[at + 512 : at + 576, cols] = part
+                wb[at + 1024 : at + 1088, cols] = jnp.where(inside, lower[x : x + 1], 0.0).astype(BF16)
+        tbuf[...] = jnp.dot(ub[...], wb[...], preferred_element_type=F32)
         for t in range(8):
             row = slice(t, t + 1)
-            wz = jnp.where(sub8 == zs[row], 1.0 - fzs[row], jnp.where(sub8 == zs[row] + 1, fzs[row], 0.0))
-            wys = []
-            for y in range(8):
-                wy = jnp.where(ys[row] == y, 1.0 - fys[row], jnp.where(ys[row] + 1 == y, fys[row], 0.0))
-                wys.append(wy * wz)
+            wz = along(zs, fzs, row)
+            wy = along(ys, fys, row)
+            wys = [wy[y : y + 1] * wz for y in range(8)]
             values = []
             for var in range(8):
                 total = None
@@ -161,17 +200,7 @@
             near_by = jnp.minimum(me, REACH) + jnp.minimum(nb - 1 - me, REACH)
             pl.semaphore_wait(barrier, nb + near_by)
 
-        @pl.loop(1, nb + 1)
-        def _(i):
-            q = lax.rem(me + i, nb)
-            pltpu.make_async_remote_copy(
-                src_ref=msg.at[half, q],
-                dst_ref=recv.at[half, me],
-                send_sem=a_send.at[half],
-                recv_sem=a_recv.at[half],
-                device_id=(1 - comp, q),
-                device_id_type=MESH,
-            ).start()
+        send_values(half)
 
     targets = tgt[...]
     tx = (targets >> 6) & 7
@@ -185,8 +214,11 @@
             lanes512 == columns[:, s : s + 1], 1.0, 0.0
         ).astype(BF16)
 
-    links = nbr[...]
-    links_c = jnp.concatenate([links.astype(F32), jnp.zeros((120, 128), F32)], axis=0).T.astype(I32)
+    links[...] = jnp.full_like(links, -1)
+    for f in range(6):
+        links[f : f + 1, 0:64] = nbr[f]
+        links[f : f + 1, 64:128] = nbr[f]
+    links_c = jnp.concatenate([links[...].astype(F32), jnp.zeros((120, 128), F32)], axis=0).T.astype(I32)
     upper_lanes = lane >> 6
     half_lane = lane & 63
     group = (half_lane * 43) >> 8
@@ -236,29 +268,28 @@
                 off != 0, slot * 6 + rank * 2 + side + (0 if high else 64), -1
             )
 
-    rows64 = lax.broadcasted_iota(I32, (64, 128), 0)
+    acc[...] = jnp.zeros_like(acc)
     for half in range(2):
         whole = recv.at[half, pl.ds(0, nb)]
         pltpu.make_async_copy(whole, whole, a_recv.at[half]).wait()
         vbuf[128 * half : 128 * half + 128, :] = recv[half].reshape(128, 128).T
-    acc[...] = jnp.zeros_like(acc)
-
-    @pl.loop(0, 4)
-    def _(g):
-        places = tgt[pl.ds(pl.multiple_of(g * 8, 8), 8), :] & 63
-        for t in range(8):
-            value = vbuf[pl.ds(pl.multiple_of(g * 64 + t * 8, 8), 8), :]
-            upper = value.astype(BF16).astype(F32)
-            lower = value - upper
-            here = rows64 == places[t : t + 1]
-            cols = slice(128 * t, 128 * t + 128)
-            for var in range(8):
-                pbuf[64 * var : 64 * var + 64, cols] = jnp.where(here, upper[var : var + 1], 0.0).astype(BF16)
-                pbuf[512 + 64 * var : 576 + 64 * var, cols] = jnp.where(here, lower[var : var + 1], 0.0).astype(BF16)
-            pbuf[1024:1088, cols] = jnp.where(here, 1.0, 0.0).astype(BF16)
-        acc[...] += jnp.dot(
-            pbuf[...], oa[pl.ds(pl.multiple_of(g * 1024, 1024), 1024), :], preferred_element_type=F32
-        )
+
+        @pl.loop(2 * half, 2 * half + 2)
+        def _(g):
+            places = tgt[pl.ds(pl.multiple_of(g * 8, 8), 8), :] & 63
+            for t in range(8):
+                value = vbuf[pl.ds(pl.multiple_of(g * 64 + t * 8, 8), 8), :]
+                upper = value.astype(BF16).astype(F32)
+                lower = value - upper
+                here = rows64 == places[t : t + 1]
+                cols = slice(128 * t, 128 * t + 128)
+                for var in range(8):
+                    pbuf[64 * var : 64 * var + 64, cols] = jnp.where(here, upper[var : var + 1], 0.0).astype(BF16)
+                    pbuf[512 + 64 * var : 576 + 64 * var, cols] = jnp.where(here, lower[var : var + 1], 0.0).astype(BF16)
+                pbuf[1024:1088, cols] = jnp.where(here, 1.0, 0.0).astype(BF16)
+            acc[...] += jnp.dot(
+                pbuf[...], oa[pl.ds(pl.multiple_of(g * 1024, 1024), 1024), :], preferred_element_type=F32
+            )
 
     for xl in range(4):
         cols = slice(128 * xl, 128 * xl + 128)
@@ -266,12 +297,12 @@
         for var in range(8):
             rows = slice(64 * var, 64 * var + 64)
             lower = slice(512 + 64 * var, 576 + 64 * var)
-            u[xl, var] = jnp.where(changed, acc[rows, cols] + acc[lower, cols], u[xl, var])
+            cur[xl, var] = jnp.where(changed, acc[rows, cols] + acc[lower, cols], cur[xl, var])
     for half in range(2):
         whole = msg.at[half, pl.ds(0, nb)]
         pltpu.make_async_copy(whole, whole, a_send.at[half]).wait()
 
-    rates = rate[...]
+    rates = jnp.concatenate([rate[...], rate[...]], axis=1)
     low_lanes = lane_iota(8) < 64
     swap = functools.partial(pltpu.roll, shift=64, axis=1)
 
@@ -296,15 +327,15 @@
                 for var in range(8):
                     at = slice(64 * xl + 8 * var, 64 * xl + 8 * var + 8)
                     if pair == 1:
-                        ft[2, at, :] = u[xl, var, 0:8, :]
-                        ft[3, at, :] = u[xl, var, 56:64, :]
+                        ft[2, at, :] = cur[xl, var, 0:8, :]
+                        ft[3, at, :] = cur[xl, var, 56:64, :]
                     elif pair == 2:
-                        ft[4, at, :] = u[xl, var, pl.ds(0, 8, stride=8), :]
-                        ft[5, at, :] = u[xl, var, pl.ds(7, 8, stride=8), :]
+                        ft[4, at, :] = cur[xl, var, pl.ds(0, 8, stride=8), :]
+                        ft[5, at, :] = cur[xl, var, pl.ds(7, 8, stride=8), :]
             if pair == 0:
                 for var in range(8):
                     ft[var // 4, 64 * (var % 4) : 64 * (var % 4) + 64, :] = jnp.where(
-                        lane < 64, u[0, var], u[3, var]
+                        lane < 64, cur[0, var], cur[3, var]
                     )
             take = idx[pair : pair + 1, :]
             packed = jnp.where(lane < 64, take_lanes(ft[2 * pair], take), take_lanes(ft[2 * pair + 1], take))
@@ -323,7 +354,9 @@
         @pl.loop(0, 8)
         def _(y):
             for xl in range(4):
-                cells = [u[xl, var, tile(y), :] for var in range(8)]
+                cells = [cur[xl, var, tile(y), :] for var in range(8)]
+                for var in range(8):
+                    old[xl, var, tile(y), :] = cells[var]
                 prim = primitives(cells)
                 for d in range(3):
                     flux, speed = half_flux(cells, prim, d)
@@ -347,7 +380,7 @@
                 sz = fs[2, xl, 8, here, :]
                 mz.append(jnp.maximum(sz, pltpu.roll(sz, 7, 0)))
             for c in range(8):
-                state = [u[xl, c, here, :] for xl in range(4)]
+                state = [old[xl, c, here, :] for xl in range(4)]
                 fx = [fs[0, xl, c, here, :] for xl in range(4)]
                 hx = []
                 for xl in range(3):
@@ -358,7 +391,7 @@
                     change = hx[xl] - (hx[xl - 1] if xl else swap(hx[3]))
                     up = (
                         fs[1, xl, c, here, :] + fs[1, xl, c, above, :]
-                        - my[xl] * (u[xl, c, above, :] - state[xl])
+                        - my[xl] * (old[xl, c, above, :] - state[xl])
                     ) * keep_y
                     change = change + (up - hy[xl, c])
                     hy[xl, c] = up
@@ -366,7 +399,7 @@
                     right = fz + pltpu.roll(fz, 7, 0) - mz[xl] * (pltpu.roll(state[xl], 7, 0) - state[xl])
                     right = jnp.where(keep_z, right, 0.0)
                     change = change + (right - pltpu.roll(right, 1, 0))
-                    u[xl, c, here, :] = state[xl] - rates * change
+                    cur[xl, c, here, :] = state[xl] - rates * change
 
         def edge(own, ghost, d, sign):
             own_flux, own_speed = half_flux(own, primitives(own), d)
@@ -405,8 +438,8 @@
                     ghost = [gb[c // 4, pl.ds(pl.multiple_of(64 * (c % 4) + y * 8, 8), 8), :] for c in range(8)]
                     delta = edge(own, ghost, 0, jnp.where(low_lanes, 1.0, -1.0))
                     for c in range(8):
-                        u[0, c, tile(y), :] = u[0, c, tile(y), :] + jnp.where(low_lanes, delta[c], 0.0)
-                        u[3, c, tile(y), :] = u[3, c, tile(y), :] + jnp.where(low_lanes, 0.0, delta[c])
+                        cur[0, c, tile(y), :] = cur[0, c, tile(y), :] + jnp.where(low_lanes, delta[c], 0.0)
+                        cur[3, c, tile(y), :] = cur[3, c, tile(y), :] + jnp.where(low_lanes, 0.0, delta[c])
             else:
                 for high in range(2):
                     at = 5 + 6 * (pair - 1) + 3 * high
@@ -428,7 +461,7 @@
                                 part = slice(56, 64) if high else slice(0, 8)
                             else:
                                 part = pl.ds(7 if high else 0, 8, stride=8)
-                            u[xl, c, part, :] = u[xl, c, part, :] + delta[c]
+                            cur[xl, c, part, :] = cur[xl, c, part, :] + delta[c]
 
         for pair in range(3):
             for o in range(8):
@@ -438,7 +471,7 @@
 
     for var in range(8):
         for j in range(2):
-            turned = jnp.concatenate([u[2 * j, var], u[2 * j + 1, var]], axis=0).T
+            turned = jnp.concatenate([cur[2 * j, var], cur[2 * j + 1, var]], axis=0).T
             out[var, :, 128 * j : 128 * j + 128] = turned[0:64]
             out[var, :, 128 * j + 256 : 128 * j + 384] = turned[64:128]
 
@@ -448,21 +481,25 @@
     cell = jnp.pad(shell_cell[0, 0].T, ((0, 0), (0, extra)))
     frac = jnp.pad(shell_frac[0, :, 0].transpose(0, 2, 1), ((0, 0), (0, 0), (0, extra)))
     target = jnp.pad(shell_target[0, 0].T, ((0, 0), (0, extra)), constant_values=64 * 512)
-    links = neighbours[0].T
-    links = jnp.pad(jnp.concatenate([links, links], axis=1), ((0, 2), (0, 0)), constant_values=-1)
-    rates = jnp.concatenate([block_rate, block_rate], axis=1)
+    links = neighbours.transpose(2, 0, 1)
     vmem = pl.BlockSpec(memory_space=pltpu.VMEM)
     result = pl.pallas_call(
         functools.partial(kernel, nb),
         out_shape=jax.ShapeDtypeStruct((8, 64, 512), F32),
-        in_specs=[vmem] * 6,
+        in_specs=[pl.BlockSpec(memory_space=pltpu.HBM)] * 6,
         out_specs=vmem,
         scratch_shapes=[
+            pltpu.VMEM((8, 64, 512), F32),
+            pltpu.VMEM((1, 64), F32),
+            pltpu.VMEM((6, 1, 64), I32),
+            pltpu.VMEM((SLOTS, 128), I32),
+            pltpu.VMEM((3, SLOTS, 128), F32),
+            pltpu.VMEM((SLOTS, 128), I32),
+            pltpu.VMEM((8, 128), I32),
+            pltpu.SemaphoreType.DMA((6,)),
             pltpu.VMEM((4, 8, 64, 128), F32),
-            pltpu.VMEM((512, 512), BF16),
-            pltpu.VMEM((512, 512), BF16),
-            pltpu.VMEM((512, 1024), BF16),
-            pltpu.VMEM((512, 1024), BF16),
+            pltpu.VMEM((512, 1536), BF16),
+            pltpu.VMEM((1536, 1024), BF16),
             pltpu.VMEM((512, 1024), F32),
             pltpu.VMEM((256, 128), F32),
             pltpu.VMEM((2, 128, 1, 128), F32),
@@ -472,6 +509,7 @@
             pltpu.VMEM((1088, 512), F32),
             pltpu.VMEM((3, 4, 9, 64, 128), F32),
             pltpu.VMEM((4, 8, 8, 128), F32),
+            pltpu.VMEM((4, 8, 64, 128), F32),
             pltpu.VMEM((6, 256, 128), F32),
             pltpu.VMEM((2, 256, 128), F32),
             pltpu.VMEM((3, 8, 24, 128), F32),
@@ -486,7 +524,7 @@
         compiler_params=pltpu.CompilerParams(
             collective_id=0, has_side_effects=True, vmem_limit_bytes=48 << 20
         ),
-    )(conserved[0], rates, links, cell, frac, target)
+    )(*(pltpu.with_memory_space_constraint(x, pltpu.HBM) for x in (conserved[0], block_rate, links, cell, frac, target)))
     return result[None]
 
 

time: 76 us -> 66.3 us (0.87)
  Pallas kernels: 71.2 us -> 65.3 us
  local copies, waits for them, and re-layouts: 4.34 us -> 0.97 us
    pallas_call x1, Pallas kernels: 71.2 us -> 65.3 us  [on_device(): pl.pallas_call(functools.partial(kernel, nb), out_shape=jax.ShapeDtypeStr...]
    unnamed x12 -> x1, local copies, waits for them, and re-layouts: 4.33 us -> 0.97 us
where the time goes in v2:
time: 66.3 us
  Pallas kernels  65.3 us (98%)
  local copies, waits for them, and re-layouts  0.97 us (1%)
    pallas_call x1, Pallas kernels, on_device(): pl.pallas_call(functools.partial(kernel, nb), out_shape=jax.ShapeDtypeStr...  65.3 us

profile of v2, /device:TPU:2, one launch (start us, length us, event | category | flops | bytes accessed | tf_op | source)
XLA Modules:
  0.0 66.3 jit_solution(17203030305826271234)
XLA Ops:
  0.0 65.3 %shard_map.64 = f32[8,64,512]{2,1,0:T(8,128)S(1)} custom-call(f32[8,64,512]{2,1,0:T(8,128)} %bitcast.13, f32[1,64]{1,0:T(1,128)} %rate_hbm.1, s32[6,1,64]{2,1,0:T(1,128)} %bitcast.17, s32[32,128]{1,0:T(8,128)} %bitcast.15, f32[3,32,128]{2,1,0:T(8,128)} %bitcast.14, s32[32,128]{1,0:T(8,128)} %bitcast.16), custom_call_target="tpu_custom_call" | custom-call | tf_op jit(solution)/shard_map/pallas_call | solution.py:486
  65.3 1.0 %copy.8 = f32[1,8,64,512]{3,2,1,0:T(8,128)} copy(f32[1,8,64,512]{3,2,1,0:T(8,128)S(1)} %bitcast.12) | data formatting | bytes 2097152

commit v3 on v2

--- a/solution.py
+++ b/solution.py
@@ -61,7 +61,7 @@
 def kernel(
     nb, cons_hbm, rate_hbm, nbr_hbm, cell_hbm, frac_hbm, tgt_hbm, out,
     cons, rate, nbr, cell, frac, tgt, links, in_sem,
-    cur, ub, wb, tbuf, vbuf, msg, recv, oa, pbuf, acc,
+    cur, ub, wb, tbuf, vbuf, msg_a, msg_b, msg_c, recv_a, recv_b, recv_c, oa, pbuf, acc,
     fs, hy, old, ft, gb, sb, hrecv, rt, idx,
     a_send, a_recv, h_send, h_recv,
 ):
@@ -82,7 +82,8 @@
         load.start()
 
     if nb < 128:
-        recv[...] = jnp.zeros_like(recv)
+        for received in (recv_a, recv_b, recv_c):
+            received[...] = jnp.zeros_like(received)
     rt[...] = jnp.zeros_like(rt)
 
     @pl.loop(0, STEPS)
@@ -117,13 +118,15 @@
                 ub[rows, at + 512 : at + 640] = (part - upper.astype(F32)).astype(BF16)
                 ub[rows, at + 1024 : at + 1152] = upper
 
-    def send_values(half):
+    pieces = (((0, 2), msg_a, recv_a), ((2, 3), msg_b, recv_b), ((3, 4), msg_c, recv_c))
+
+    def send_values(piece):
         def send(q):
             pltpu.make_async_remote_copy(
-                src_ref=msg.at[half, q],
-                dst_ref=recv.at[half, me],
-                send_sem=a_send.at[half],
-                recv_sem=a_recv.at[half],
+                src_ref=pieces[piece][1].at[q],
+                dst_ref=pieces[piece][2].at[me],
+                send_sem=a_send.at[piece],
+                recv_sem=a_recv.at[piece],
                 device_id=(1 - comp, q),
                 device_id_type=MESH,
             ).start()
@@ -190,17 +193,17 @@
                 values.append(jnp.sum(total, axis=0, keepdims=True))
             vbuf[pl.ds(pl.multiple_of(g * 64 + t * 8, 8), 8), :] = jnp.concatenate(values, axis=0)
 
-    for half in range(2):
-        @pl.loop(2 * half, 2 * half + 2)
+    for piece, ((first, last), message, _) in enumerate(pieces):
+        @pl.loop(first, last)
         def _(g):
             interpolate(g)
 
-        msg[half] = vbuf[128 * half : 128 * half + 128, :].T.reshape(128, 1, 128)
-        if half == 0:
+        message[...] = vbuf[64 * first : 64 * last, :].T.reshape(message.shape)
+        if piece == 0:
             near_by = jnp.minimum(me, REACH) + jnp.minimum(nb - 1 - me, REACH)
             pl.semaphore_wait(barrier, nb + near_by)
 
-        send_values(half)
+        send_values(piece)
 
     targets = tgt[...]
     tx = (targets >> 6) & 7
@@ -269,12 +272,12 @@
             )
 
     acc[...] = jnp.zeros_like(acc)
-    for half in range(2):
-        whole = recv.at[half, pl.ds(0, nb)]
-        pltpu.make_async_copy(whole, whole, a_recv.at[half]).wait()
-        vbuf[128 * half : 128 * half + 128, :] = recv[half].reshape(128, 128).T
-
-        @pl.loop(2 * half, 2 * half + 2)
+    for piece, ((first, last), _, received) in enumerate(pieces):
+        whole = received.at[pl.ds(0, nb)]
+        pltpu.make_async_copy(whole, whole, a_recv.at[piece]).wait()
+        vbuf[64 * first : 64 * last, :] = received[...].reshape(128, 64 * (last - first)).T
+
+        @pl.loop(first, last)
         def _(g):
             places = tgt[pl.ds(pl.multiple_of(g * 8, 8), 8), :] & 63
             for t in range(8):
@@ -286,21 +289,20 @@
                 for var in range(8):
                     pbuf[64 * var : 64 * var + 64, cols] = jnp.where(here, upper[var : var + 1], 0.0).astype(BF16)
                     pbuf[512 + 64 * var : 576 + 64 * var, cols] = jnp.where(here, lower[var : var + 1], 0.0).astype(BF16)
-                pbuf[1024:1088, cols] = jnp.where(here, 1.0, 0.0).astype(BF16)
             acc[...] += jnp.dot(
                 pbuf[...], oa[pl.ds(pl.multiple_of(g * 1024, 1024), 1024), :], preferred_element_type=F32
             )
 
     for xl in range(4):
         cols = slice(128 * xl, 128 * xl + 128)
-        changed = acc[1024:1088, cols] > 0.5
+        changed = acc[0:64, cols] + acc[512:576, cols] > 0.25
         for var in range(8):
             rows = slice(64 * var, 64 * var + 64)
             lower = slice(512 + 64 * var, 576 + 64 * var)
             cur[xl, var] = jnp.where(changed, acc[rows, cols] + acc[lower, cols], cur[xl, var])
-    for half in range(2):
-        whole = msg.at[half, pl.ds(0, nb)]
-        pltpu.make_async_copy(whole, whole, a_send.at[half]).wait()
+    for piece, (_, message, _) in enumerate(pieces):
+        whole = message.at[pl.ds(0, nb)]
+        pltpu.make_async_copy(whole, whole, a_send.at[piece]).wait()
 
     rates = jnp.concatenate([rate[...], rate[...]], axis=1)
     low_lanes = lane_iota(8) < 64
@@ -401,14 +403,25 @@
                     change = change + (right - pltpu.roll(right, 1, 0))
                     cur[xl, c, here, :] = state[xl] - rates * change
 
-        def edge(own, ghost, d, sign):
-            own_flux, own_speed = half_flux(own, primitives(own), d)
+        def edge(own, own_flux, own_speed, ghost, d, sign):
             far_flux, far_speed = half_flux(ghost, primitives(ghost), d)
             most = jnp.maximum(own_speed, far_speed)
             return [
                 rates * (sign * (own_flux[c] + far_flux[c]) - most * (own[c] - ghost[c]))
                 for c in range(8)
             ]
+
+        for s in range(2):
+            gb[s] = take_lanes(ft[s], idx[3:4, :])
+        for pair in (1, 2):
+            for high in range(2):
+                at = 5 + 6 * (pair - 1) + 3 * high
+                near = idx[at : at + 1, :]
+                gb[2 * pair + high] = jnp.where(
+                    near >= 0,
+                    take_lanes(ft[2 * pair + 1 - high], jnp.maximum(near, 0)),
+                    ft[2 * pair + high],
+                )
 
         for pair in range(3):
             for o in range(8):
@@ -423,44 +436,40 @@
                         ]
             arrived = jnp.concatenate([rt[0].T, rt[1].T], axis=0)
             if pair == 0:
-                near = idx[3:4, :]
                 far = idx[4:5, :]
                 for s in range(2):
                     gb[s] = jnp.where(
                         far >= 0,
                         take_lanes(arrived, jnp.maximum(far, 0) + 64 * s),
-                        take_lanes(ft[s], near),
+                        gb[s],
                     )
 
                 @pl.loop(0, 8)
                 def _(y):
                     own = [ft[c // 4, pl.ds(pl.multiple_of(64 * (c % 4) + y * 8, 8), 8), :] for c in range(8)]
                     ghost = [gb[c // 4, pl.ds(pl.multiple_of(64 * (c % 4) + y * 8, 8), 8), :] for c in range(8)]
-                    delta = edge(own, ghost, 0, jnp.where(low_lanes, 1.0, -1.0))
+                    flux = [jnp.where(low_lanes, fs[0, 0, c, tile(y), :], fs[0, 3, c, tile(y), :]) for c in range(9)]
+                    delta = edge(own, flux[:8], flux[8], ghost, 0, jnp.where(low_lanes, 1.0, -1.0))
                     for c in range(8):
                         cur[0, c, tile(y), :] = cur[0, c, tile(y), :] + jnp.where(low_lanes, delta[c], 0.0)
                         cur[3, c, tile(y), :] = cur[3, c, tile(y), :] + jnp.where(low_lanes, 0.0, delta[c])
             else:
                 for high in range(2):
                     at = 5 + 6 * (pair - 1) + 3 * high
-                    near = idx[at : at + 1, :]
                     far = idx[at + 1 : at + 2, :]
-                    local = jnp.where(
-                        near >= 0,
-                        take_lanes(ft[2 * pair + 1 - high], jnp.maximum(near, 0)),
-                        ft[2 * pair + high],
-                    )
-                    gb[high] = jnp.where(far >= 0, take_lanes(arrived, jnp.maximum(far, 0)), local)
+                    mine = 2 * pair + high
+                    gb[mine] = jnp.where(far >= 0, take_lanes(arrived, jnp.maximum(far, 0)), gb[mine])
+                    if pair == 1:
+                        part = slice(56, 64) if high else slice(0, 8)
+                    else:
+                        part = pl.ds(7 if high else 0, 8, stride=8)
                     for xl in range(4):
                         rows = [slice(64 * xl + 8 * c, 64 * xl + 8 * c + 8) for c in range(8)]
-                        own = [ft[2 * pair + high, rows[c], :] for c in range(8)]
-                        ghost = [gb[high, rows[c], :] for c in range(8)]
-                        delta = edge(own, ghost, pair, -1.0 if high else 1.0)
+                        own = [ft[mine, rows[c], :] for c in range(8)]
+                        ghost = [gb[mine, rows[c], :] for c in range(8)]
+                        flux = [fs[pair, xl, c, part, :] for c in range(9)]
+                        delta = edge(own, flux[:8], flux[8], ghost, pair, -1.0 if high else 1.0)
                         for c in range(8):
-                            if pair == 1:
-                                part = slice(56, 64) if high else slice(0, 8)
-                            else:
-                                part = pl.ds(7 if high else 0, 8, stride=8)
                             cur[xl, c, part, :] = cur[xl, c, part, :] + delta[c]
 
         for pair in range(3):
@@ -502,22 +511,26 @@
             pltpu.VMEM((1536, 1024), BF16),
             pltpu.VMEM((512, 1024), F32),
             pltpu.VMEM((256, 128), F32),
-            pltpu.VMEM((2, 128, 1, 128), F32),
-            pltpu.VMEM((2, 128, 1, 128), F32),
+            pltpu.VMEM((128, 1, 128), F32),
+            pltpu.VMEM((128, 1, 64), F32),
+            pltpu.VMEM((128, 1, 64), F32),
+            pltpu.VMEM((128, 1, 128), F32),
+            pltpu.VMEM((128, 1, 64), F32),
+            pltpu.VMEM((128, 1, 64), F32),
             pltpu.VMEM((4096, 512), BF16),
-            pltpu.VMEM((1088, 1024), BF16),
-            pltpu.VMEM((1088, 512), F32),
+            pltpu.VMEM((1024, 1024), BF16),
+            pltpu.VMEM((1024, 512), F32),
             pltpu.VMEM((3, 4, 9, 64, 128), F32),
             pltpu.VMEM((4, 8, 8, 128), F32),
             pltpu.VMEM((4, 8, 64, 128), F32),
             pltpu.VMEM((6, 256, 128), F32),
-            pltpu.VMEM((2, 256, 128), F32),
+            pltpu.VMEM((6, 256, 128), F32),
             pltpu.VMEM((3, 8, 24, 128), F32),
             pltpu.VMEM((STEPS, 3, 8, 24, 128), F32),
             pltpu.VMEM((2, 128, 128), F32),
             pltpu.VMEM((24, 128), I32),
-            pltpu.SemaphoreType.DMA((2,)),
-            pltpu.SemaphoreType.DMA((2,)),
+            pltpu.SemaphoreType.DMA((3,)),
+            pltpu.SemaphoreType.DMA((3,)),
             pltpu.SemaphoreType.DMA((STEPS, 3, 8)),
             pltpu.SemaphoreType.DMA((STEPS, 3, 8)),
         ],

time: 66.3 us -> 65.7 us (level)
  no operation moved by 1% of the time
where the time goes in v3:
time: 65.7 us
  Pallas kernels  64.7 us (98%)
  local copies, waits for them, and re-layouts  0.97 us (1%)
    pallas_call x1, Pallas kernels, on_device(): pl.pallas_call(functools.partial(kernel, nb), out_shape=jax.ShapeDtypeStr...  64.7 us

profile of v3, /device:TPU:2, one launch (start us, length us, event | category | flops | bytes accessed | tf_op | source)
XLA Modules:
  0.0 65.7 jit_solution(7111236691620058791)
XLA Ops:
  0.0 64.7 %shard_map.64 = f32[8,64,512]{2,1,0:T(8,128)S(1)} custom-call(f32[8,64,512]{2,1,0:T(8,128)} %bitcast.13, f32[1,64]{1,0:T(1,128)} %rate_hbm.1, s32[6,1,64]{2,1,0:T(1,128)} %bitcast.17, s32[32,128]{1,0:T(8,128)} %bitcast.15, f32[3,32,128]{2,1,0:T(8,128)} %bitcast.14, s32[32,128]{1,0:T(8,128)} %bitcast.16), custom_call_target="tpu_custom_call" | custom-call | tf_op jit(solution)/shard_map/pallas_call | solution.py:495
  64.7 1.0 %copy.8 = f32[1,8,64,512]{3,2,1,0:T(8,128)} copy(f32[1,8,64,512]{3,2,1,0:T(8,128)S(1)} %bitcast.12) | data formatting | bytes 2097152

commit v4 on v3

--- a/solution.py
+++ b/solution.py
@@ -61,7 +61,7 @@
 def kernel(
     nb, cons_hbm, rate_hbm, nbr_hbm, cell_hbm, frac_hbm, tgt_hbm, out,
     cons, rate, nbr, cell, frac, tgt, links, in_sem,
-    cur, ub, wb, tbuf, vbuf, msg_a, msg_b, msg_c, recv_a, recv_b, recv_c, oa, pbuf, acc,
+    cur, ub, wb, tbuf, vbuf, msg_a, msg_b, recv_a, recv_b, oa, pbuf, acc,
     fs, hy, old, ft, gb, sb, hrecv, rt, idx,
     a_send, a_recv, h_send, h_recv,
 ):
@@ -82,7 +82,7 @@
         load.start()
 
     if nb < 128:
-        for received in (recv_a, recv_b, recv_c):
+        for received in (recv_a, recv_b):
             received[...] = jnp.zeros_like(received)
     rt[...] = jnp.zeros_like(rt)
 
@@ -118,7 +118,7 @@
                 ub[rows, at + 512 : at + 640] = (part - upper.astype(F32)).astype(BF16)
                 ub[rows, at + 1024 : at + 1152] = upper
 
-    pieces = (((0, 2), msg_a, recv_a), ((2, 3), msg_b, recv_b), ((3, 4), msg_c, recv_c))
+    pieces = (((0, 2), msg_a, recv_a), ((2, 4), msg_b, recv_b))
 
     def send_values(piece):
         def send(q):
@@ -193,17 +193,17 @@
                 values.append(jnp.sum(total, axis=0, keepdims=True))
             vbuf[pl.ds(pl.multiple_of(g * 64 + t * 8, 8), 8), :] = jnp.concatenate(values, axis=0)
 
-    for piece, ((first, last), message, _) in enumerate(pieces):
-        @pl.loop(first, last)
-        def _(g):
-            interpolate(g)
-
-        message[...] = vbuf[64 * first : 64 * last, :].T.reshape(message.shape)
-        if piece == 0:
-            near_by = jnp.minimum(me, REACH) + jnp.minimum(nb - 1 - me, REACH)
-            pl.semaphore_wait(barrier, nb + near_by)
-
-        send_values(piece)
+    @pl.loop(0, 4)
+    def _(g):
+        interpolate(g)
+        for piece, ((first, last), message, _) in enumerate(pieces):
+            @pl.when(g == last - 1)
+            def _():
+                message[...] = vbuf[64 * first : 64 * last, :].T.reshape(message.shape)
+                if piece == 0:
+                    near_by = jnp.minimum(me, REACH) + jnp.minimum(nb - 1 - me, REACH)
+                    pl.semaphore_wait(barrier, nb + near_by)
+                send_values(piece)
 
     targets = tgt[...]
     tx = (targets >> 6) & 7
@@ -272,26 +272,28 @@
             )
 
     acc[...] = jnp.zeros_like(acc)
-    for piece, ((first, last), _, received) in enumerate(pieces):
-        whole = received.at[pl.ds(0, nb)]
-        pltpu.make_async_copy(whole, whole, a_recv.at[piece]).wait()
-        vbuf[64 * first : 64 * last, :] = received[...].reshape(128, 64 * (last - first)).T
-
-        @pl.loop(first, last)
-        def _(g):
-            places = tgt[pl.ds(pl.multiple_of(g * 8, 8), 8), :] & 63
-            for t in range(8):
-                value = vbuf[pl.ds(pl.multiple_of(g * 64 + t * 8, 8), 8), :]
-                upper = value.astype(BF16).astype(F32)
-                lower = value - upper
-                here = rows64 == places[t : t + 1]
-                cols = slice(128 * t, 128 * t + 128)
-                for var in range(8):
-                    pbuf[64 * var : 64 * var + 64, cols] = jnp.where(here, upper[var : var + 1], 0.0).astype(BF16)
-                    pbuf[512 + 64 * var : 576 + 64 * var, cols] = jnp.where(here, lower[var : var + 1], 0.0).astype(BF16)
-            acc[...] += jnp.dot(
-                pbuf[...], oa[pl.ds(pl.multiple_of(g * 1024, 1024), 1024), :], preferred_element_type=F32
-            )
+    @pl.loop(0, 4)
+    def _(g):
+        for piece, ((first, last), _, received) in enumerate(pieces):
+            @pl.when(g == first)
+            def _():
+                whole = received.at[pl.ds(0, nb)]
+                pltpu.make_async_copy(whole, whole, a_recv.at[piece]).wait()
+                vbuf[64 * first : 64 * last, :] = received[...].reshape(128, 64 * (last - first)).T
+
+        places = tgt[pl.ds(pl.multiple_of(g * 8, 8), 8), :] & 63
+        for t in range(8):
+            value = vbuf[pl.ds(pl.multiple_of(g * 64 + t * 8, 8), 8), :]
+            upper = value.astype(BF16).astype(F32)
+            lower = value - upper
+            here = rows64 == places[t : t + 1]
+            cols = slice(128 * t, 128 * t + 128)
+            for var in range(8):
+                pbuf[64 * var : 64 * var + 64, cols] = jnp.where(here, upper[var : var + 1], 0.0).astype(BF16)
+                pbuf[512 + 64 * var : 576 + 64 * var, cols] = jnp.where(here, lower[var : var + 1], 0.0).astype(BF16)
+        acc[...] += jnp.dot(
+            pbuf[...], oa[pl.ds(pl.multiple_of(g * 1024, 1024), 1024), :], preferred_element_type=F32
+        )
 
     for xl in range(4):
         cols = slice(128 * xl, 128 * xl + 128)
@@ -311,13 +313,20 @@
     def copy_of(step, pair, o):
         offset = OFFSETS[o]
         return pltpu.make_async_remote_copy(
-            src_ref=sb.at[pair, o],
+            src_ref=sb.at[step, pair, o],
             dst_ref=hrecv.at[step, pair, OFFSETS.index(-offset)],
             send_sem=h_send.at[step, pair, o],
             recv_sem=h_recv.at[step, pair, OFFSETS.index(-offset)],
             device_id=(comp, me + offset),
             device_id_type=MESH,
         )
+
+    def sent(step):
+        for pair in range(3):
+            for o in range(8):
+                @pl.when(exists(OFFSETS[o]))
+                def _():
+                    copy_of(step, pair, o).wait_send()
 
     def tile(y):
         return pl.ds(pl.multiple_of(y * 8, 8), 8)
@@ -345,7 +354,7 @@
                 turned = packed[128 * r : 128 * r + 128].T
                 for o in range(8):
                     for s in range(2):
-                        sb[pair, o, 12 * s + 6 * r : 12 * s + 6 * r + 6, :] = turned[
+                        sb[step, pair, o, 12 * s + 6 * r : 12 * s + 6 * r + 6, :] = turned[
                             64 * s + 6 * o : 64 * s + 6 * o + 6
                         ]
             for o in SEND_ORDER:
@@ -411,6 +420,10 @@
                 for c in range(8)
             ]
 
+        @pl.when(step > 0)
+        def _():
+            sent(step - 1)
+
         for s in range(2):
             gb[s] = take_lanes(ft[s], idx[3:4, :])
         for pair in (1, 2):
@@ -472,11 +485,7 @@
                         for c in range(8):
                             cur[xl, c, part, :] = cur[xl, c, part, :] + delta[c]
 
-        for pair in range(3):
-            for o in range(8):
-                @pl.when(exists(OFFSETS[o]))
-                def _():
-                    copy_of(step, pair, o).wait_send()
+    sent(STEPS - 1)
 
     for var in range(8):
         for j in range(2):
@@ -512,11 +521,9 @@
             pltpu.VMEM((512, 1024), F32),
             pltpu.VMEM((256, 128), F32),
             pltpu.VMEM((128, 1, 128), F32),
-            pltpu.VMEM((128, 1, 64), F32),
-            pltpu.VMEM((128, 1, 64), F32),
             pltpu.VMEM((128, 1, 128), F32),
-            pltpu.VMEM((128, 1, 64), F32),
-            pltpu.VMEM((128, 1, 64), F32),
+            pltpu.VMEM((128, 1, 128), F32),
+            pltpu.VMEM((128, 1, 128), F32),
             pltpu.VMEM((4096, 512), BF16),
             pltpu.VMEM((1024, 1024), BF16),
             pltpu.VMEM((1024, 512), F32),
@@ -525,12 +532,12 @@
             pltpu.VMEM((4, 8, 64, 128), F32),
             pltpu.VMEM((6, 256, 128), F32),
             pltpu.VMEM((6, 256, 128), F32),
-            pltpu.VMEM((3, 8, 24, 128), F32),
+            pltpu.VMEM((STEPS, 3, 8, 24, 128), F32),
             pltpu.VMEM((STEPS, 3, 8, 24, 128), F32),
             pltpu.VMEM((2, 128, 128), F32),
             pltpu.VMEM((24, 128), I32),
-            pltpu.SemaphoreType.DMA((3,)),
-            pltpu.SemaphoreType.DMA((3,)),
+            pltpu.SemaphoreType.DMA((2,)),
+            pltpu.SemaphoreType.DMA((2,)),
             pltpu.SemaphoreType.DMA((STEPS, 3, 8)),
             pltpu.SemaphoreType.DMA((STEPS, 3, 8)),
         ],

time: 65.7 us -> 66.1 us (level)
  no operation moved by 1% of the time
where the time goes in v4:
time: 66.1 us; the launch traced here: 66 us
  Pallas kernels  65 us (98%)
  local copies, waits for them, and re-layouts  0.97 us (1%)
    pallas_call x1, Pallas kernels, on_device(): pl.pallas_call(functools.partial(kernel, nb), out_shape=jax.ShapeDtypeStr...  65 us

profile of v4, /device:TPU:2, one launch (start us, length us, event | category | flops | bytes accessed | tf_op | source)
XLA Modules:
  0.0 66.0 jit_solution(14310097029571486375)
XLA Ops:
  0.0 65.0 %shard_map.64 = f32[8,64,512]{2,1,0:T(8,128)S(1)} custom-call(f32[8,64,512]{2,1,0:T(8,128)} %bitcast.13, f32[1,64]{1,0:T(1,128)} %rate_hbm.1, s32[6,1,64]{2,1,0:T(1,128)} %bitcast.17, s32[32,128]{1,0:T(8,128)} %bitcast.15, f32[3,32,128]{2,1,0:T(8,128)} %bitcast.14, s32[32,128]{1,0:T(8,128)} %bitcast.16), custom_call_target="tpu_custom_call" | custom-call | tf_op jit(solution)/shard_map/pallas_call | solution.py:504
  65.0 1.0 %copy.8 = f32[1,8,64,512]{3,2,1,0:T(8,128)} copy(f32[1,8,64,512]{3,2,1,0:T(8,128)S(1)} %bitcast.12) | data formatting | bytes 2097152
